TPU v7x, 256 devices: a whole 4x4x8 slice. The times are simulated.
256 devices in a mesh: blocks: 64 (over x_lo, y, z), filt: 4 (over x_hi, core).
Axes of the slice: x: 4 (x_hi: 2, x_lo: 2; x = x_hi * 2 + x_lo), y: 4, z: 8, core: 2. Of those that a mesh axis runs over, the one named last changes fastest.
Arguments:
- volume: bfloat16 [64, 4, 512, 128], P(None, None, 'blocks'), may hold values from -6 to 6
- w_first: bfloat16 [3, 3, 64, 64], P(None, None, 'filt'), may hold values from -0.25 to 0.25
- w_second: bfloat16 [3, 3, 3, 64, 64], P(None, None, None, 'filt'), may hold values from -0.15625 to 0.15625
- cotangent: bfloat16 [64, 4, 512, 128], P('filt', None, 'blocks'), may hold values from -6 to 6
Outputs:
- output: bfloat16 [64, 4, 512, 128], P('filt', None, 'blocks')
- input_grad: bfloat16 [64, 4, 512, 128], P('filt', None, 'blocks')
- first_grad: float32 [3, 3, 64, 64], P(None, None, 'filt')
- second_grad: float32 [3, 3, 3, 64, 64], P(None, None, None, 'filt')
All inputs are finite; a program needn't handle non-finite values.
Results may differ from a plain program's by a relative error of at most 0.012.
Values may be sent and summed in bfloat16 or wider, within the bound.
No kernel may reach another device: no remote copies, remote signals or barrier semaphores. Data moves between devices by JAX's collectives and lax.ppermute only.
A program may use at most 64 MiB of HBM per device.

v0:
```python
import math

import jax
import jax.numpy as jnp
from jax import lax
from jax.sharding import PartitionSpec as P


def extended(block, sides, width):
    for axis, dim in sides:
        count = lax.axis_size(axis)
        forward = [(i, i + 1) for i in range(count - 1)]
        backward = [(target, source) for source, target in forward]
        low = lax.ppermute(
            lax.slice_in_dim(block, block.shape[dim] - width, None, axis=dim), axis, forward
        )
        high = lax.ppermute(lax.slice_in_dim(block, 0, width, axis=dim), axis, backward)
        block = jnp.concatenate([low, block, high], axis=dim)
    return block


def correlate(padded, kernel, stride, out_depth, out_rows, out_cols):
    summed = None
    for a in range(kernel.shape[0]):
        for b in range(kernel.shape[1]):
            for c in range(kernel.shape[2]):
                window = padded[
                    :,
                    a * stride : a * stride + out_depth,
                    b * stride : b * stride + out_rows,
                    c * stride : c * stride + out_cols,
                ]
                product = jnp.einsum(
                    "oi,izyx->ozyx", kernel[a, b, c], window, preferred_element_type=jnp.float32
                )
                summed = product if summed is None else summed + product
    return summed


def kernel_grads(left, padded, taps, stride):
    out_depth, out_rows, out_cols = (left.shape[1], left.shape[2], left.shape[3])
    planes = []
    for a in range(taps[0]):
        lines = []
        for b in range(taps[1]):
            entries = []
            for c in range(taps[2]):
                window = padded[
                    :,
                    a * stride : a * stride + out_depth,
                    b * stride : b * stride + out_rows,
                    c * stride : c * stride + out_cols,
                ]
                entries.append(
                    jnp.einsum("ozyx,izyx->oi", left, window, preferred_element_type=jnp.float32)
                )
            lines.append(jnp.stack(entries))
        planes.append(jnp.stack(lines))
    return jnp.stack(planes)


def flipped(kernel):
    return jnp.swapaxes(jnp.flip(kernel, axis=(0, 1, 2)), 3, 4)


def silu_slope(pre):
    sigma = jax.nn.sigmoid(pre)
    return sigma * (1.0 + pre * (1.0 - sigma))


def per_device(volume, w_first, w_second, cotangent):
    z_cells, y_rows, x_cells = (volume.shape[1], volume.shape[2], volume.shape[3])
    block_count = lax.axis_size("blocks")
    first_kernel = w_first[None]
    volume_halo = extended(volume, (("blocks", 2),), 1)
    volume_pad = jnp.pad(volume_halo, ((0, 0), (0, 0), (0, 0), (1, 1)))
    pre = correlate(volume_pad, first_kernel, 1, z_cells, y_rows, x_cells)
    hidden = jax.nn.silu(pre).astype(jnp.bfloat16)
    hidden_all = lax.all_gather(hidden, "filt", axis=0, tiled=True)
    hidden_rim = extended(hidden_all, (("blocks", 2),), 2)
    hidden_pad = jnp.pad(hidden_rim, ((0, 0), (2, 2), (0, 0), (2, 2)))
    output = correlate(hidden_pad, w_second, 2, z_cells, y_rows, x_cells).astype(jnp.bfloat16)
    second_local = kernel_grads(cotangent, hidden_pad, (3, 3, 3), 2)
    grad_rim = extended(cotangent, (("blocks", 2),), 2)
    grad_pad = jnp.pad(grad_rim, ((0, 0), (2, 2), (0, 0), (2, 2)))
    partial_hidden = correlate(grad_pad, flipped(w_second), 2, z_cells, y_rows, x_cells)
    hidden_grad = lax.psum_scatter(partial_hidden, "filt", scatter_dimension=0, tiled=True)
    pre_grad = (hidden_grad * silu_slope(pre)).astype(jnp.bfloat16)
    first_local = kernel_grads(pre_grad, volume_pad, (1, 3, 3), 1)[0]
    pre_rim = extended(pre_grad, (("blocks", 2),), 1)
    pre_pad = jnp.pad(pre_rim, ((0, 0), (0, 0), (0, 0), (1, 1)))
    partial_input = correlate(pre_pad, flipped(first_kernel), 1, z_cells, y_rows, x_cells)
    input_grad = lax.psum_scatter(
        partial_input.astype(jnp.bfloat16), "filt", scatter_dimension=0, tiled=True
    )
    factor = 1.0 / math.sqrt(z_cells * y_rows * block_count * x_cells)
    first_grad, second_grad = lax.psum((first_local * factor, second_local * factor), "blocks")
    return (output, input_grad, first_grad, second_grad)


def solution(mesh):
    return jax.shard_map(
        per_device,
        mesh=mesh,
        in_specs=(
            P(None, None, "blocks", None),
            P(None, None, "filt", None),
            P(None, None, None, "filt", None),
            P("filt", None, "blocks", None),
        ),
        out_specs=(
            P("filt", None, "blocks", None),
            P("filt", None, "blocks", None),
            P(None, None, "filt", None),
            P(None, None, None, "filt", None),
        ),
        check_vma=False,
    )
```

profile of v0, /device:TPU:4, one launch (start us, length us, event | category | flops | bytes accessed | tf_op | source)
XLA Modules:
  0.0 1009.3 jit_solution(720453746476515706)
XLA Ops:
  8.2 3.8 collective-permute-start.4
  12.0 1.3 collective-permute-start.5
  13.3 1.2 copy.8
  14.6 4.5 collective-permute-start
  19.2 1.3 collective-permute-start.1
  21.4 1.3 fusion.171
  22.7 1.2 fusion.170
  33.4 1.4 fusion.17
  37.7 2.0 fusion.309
  39.7 35.5 %reduce-scatter.3.cloned.1.call-done = f32[16,4,8,128]{3,0,2,1:T(8,128)} async-done(((f32[64,4,8,128]{3,0,2,1:T(8,128)}), f32[16,4,8,128]{3,0,2,1:T(8,128)}) %reduce-scatter.3.cloned.1.call-update) | async-done | bytes 262160 | tf_op jit(solution)/shard_map/reduce_scatter | solution.py:87
  75.2 1.2 multiply_convert_fusion
  77.3 9.1 all_gather.3
  87.5 3.5 collective-permute-start.6
  91.0 1.3 collective-permute-start.7
  92.3 4.6 collective-permute-start.2
  96.8 1.3 collective-permute-start.3
  99.7 310.2 %psum.14 = f32[3,3,16,64]{3,2,1,0:T(8,128)} all-reduce(f32[3,3,16,64]{3,2,1,0:T(8,128)S(1)} %maximum_multiply_fusion.1), channel_id=1, replica_groups=mesh['blocks'=64,'filt'=4] {'blocks'}, use_global_device_ids=true, to_apply=%region_2.3 | all-reduce | flops 9216 | bytes 73728 | tf_op jit(solution)/shard_map/psum | solution.py:97
  413.0 1.1 fusion.34
  414.6 1.7 fusion.196
  416.5 1.6 fusion.185
  418.1 2.0 select_maximum_fusion
  422.2 1.0 fusion.214
  435.9 1.1 convolution_bitcast_fusion.20
  438.8 2.8 fusion.307
  448.5 1.6 convolution_bitcast_fusion.18
  450.1 1.7 convolution_bitcast_fusion.17
  451.8 1.7 convolution_bitcast_fusion.16
  453.5 1.6 convolution_bitcast_fusion.15
  455.3 2.2 fusion.55
  459.7 1.6 copy.93
  461.3 539.8 %all-reduce.6.cloned.1.call-done = f32[3,3,3,16,64]{4,3,2,1,0:T(8,128)} async-done(((f32[3,3,3,16,64]{4,3,2,1,0:T(8,128)}), f32[3,3,3,16,64]{4,3,2,1,0:T(8,128)}) %all-reduce.6.cloned.1.call-update) | async-done | bytes 110608 | tf_op jit(solution)/shard_map/psum | solution.py:97
  1001.1 1.6 copy.351
  (185 shorter events, 46.7 us)
Async XLA Ops:
  7.2 16.7 %copy-start.23 = (bf16[3,3,16,64]{3,2,1,0:T(8,128)(2,1)S(1)}, bf16[3,3,16,64]{3,2,1,0:T(8,128)(2,1)}, u32[]{:S(2)}) copy-start(bf16[3,3,16,64]{3,2,1,0:T(8,128)(2,1)} %param.5) | copy-start | bytes 55300
  7.2 68.0 %reduce-scatter.3.cloned.1.call-start = ((), (), s32[]{:S(2)}) async-start(), calls=%async_computation.2 | async-start | bytes 1310720 | tf_op jit(solution)/shard_map/reduce_scatter | solution.py:87
  8.2 15.7 %collective-permute-start.4 = (bf16[16,4,2,128]{3,0,2,1:T(8,128)(2,1)S(1)}, bf16[16,4,2,128]{3,0,2,1:T(8,128)(2,1)S(1)}, u32[]{:S(2)}, u32[]{:S(2)}) collective-permute-start(bf16[16,4,2,128]{3,0,2,1:T(8,128)(2,1)S(1)} %get-tuple-element.50), channel_id=1, source_target_pairs={{0,4},{4,8},{8,12},{12,16},{16,20},{20,24},{24,28},{28,32},{32,36}... | collective-permute-start | bytes 98312 | tf_op jit(solution)/shard_map/ppermute | solution.py:14
  12.0 11.9 %collective-permute-start.5 = (bf16[16,4,2,128]{3,0,2,1:T(8,128)(2,1)S(1)}, bf16[16,4,2,128]{3,0,2,1:T(8,128)(2,1)S(1)}, u32[]{:S(2)}, u32[]{:S(2)}) collective-permute-start(bf16[16,4,2,128]{3,0,2,1:T(8,128)(2,1)S(1)} %get-tuple-element.51), channel_id=1, source_target_pairs={{4,0},{8,4},{12,8},{16,12},{20,16},{24,20},{28,24},{32,28},{36,32}... | collective-permute-start | bytes 98312 | tf_op jit(solution)/shard_map/ppermute | solution.py:17
  14.6 20.3 %collective-permute-start = (bf16[64,4,1,128]{3,0,2,1:T(8,128)(2,1)S(1)}, bf16[64,4,1,128]{3,0,2,1:T(8,128)(2,1)S(1)}, u32[]{:S(2)}, u32[]{:S(2)}) collective-permute-start(bf16[64,4,1,128]{3,0,2,1:T(8,128)(2,1)S(1)} %get-tuple-element.44), channel_id=1, source_target_pairs={{0,4},{4,8},{8,12},{12,16},{16,20},{20,24},{24,28},{28,32},{32,36}... | collective-permute-start | bytes 196616 | tf_op jit(solution)/shard_map/ppermute | solution.py:14
  19.2 15.7 %collective-permute-start.1 = (bf16[64,4,1,128]{3,0,2,1:T(8,128)(2,1)S(1)}, bf16[64,4,1,128]{3,0,2,1:T(8,128)(2,1)S(1)}, u32[]{:S(2)}, u32[]{:S(2)}) collective-permute-start(bf16[64,4,1,128]{3,0,2,1:T(8,128)(2,1)S(1)} %get-tuple-element.45), channel_id=1, source_target_pairs={{4,0},{8,4},{12,8},{16,12},{20,16},{24,20},{28,24},{32,28},{36,32}... | collective-permute-start | bytes 196616 | tf_op jit(solution)/shard_map/ppermute | solution.py:17
  34.8 424.9 %reduce-scatter.5.cloned.1.call-start = ((), (), s32[]{:S(2)}) async-start(), calls=%async_computation.3 | async-start | bytes 655360 | tf_op jit(solution)/shard_map/reduce_scatter | solution.py:93
  37.6 39.2 %copy-start.2 = (bf16[64,4,8,128]{3,2,1,0:T(8,128)(2,1)S(1)}, bf16[64,4,8,128]{3,2,1,0:T(8,128)(2,1)}, u32[]{:S(2)}) copy-start(bf16[64,4,8,128]{3,2,1,0:T(8,128)(2,1)} %param.4) | copy-start | bytes 1572868
  39.7 46.7 %copy-start.20 = (bf16[16,4,8,128]{3,2,1,0:T(8,128)(2,1)S(1)}, bf16[16,4,8,128]{3,2,1,0:T(8,128)(2,1)}, u32[]{:S(2)}) copy-start(bf16[16,4,8,128]{3,2,1,0:T(8,128)(2,1)} %param.7) | copy-start | bytes 393220
  75.2 22.9 %copy-start.19 = (bf16[64,4,8,128]{3,0,2,1:T(8,128)(2,1)S(1)}, bf16[64,4,8,128]{3,0,2,1:T(8,128)(2,1)}, u32[]{:S(2)}) copy-start(bf16[64,4,8,128]{3,0,2,1:T(8,128)(2,1)} %get-tuple-element.32) | copy-start | bytes 1572868
  75.2 23.2 %copy-start.18 = (bf16[64,4,8,128]{3,0,2,1:T(8,128)(2,1)S(1)}, bf16[64,4,8,128]{3,0,2,1:T(8,128)(2,1)}, u32[]{:S(2)}) copy-start(bf16[64,4,8,128]{3,0,2,1:T(8,128)(2,1)} %get-tuple-element.33) | copy-start | bytes 1572868
  76.4 22.3 %copy-start.17 = (bf16[64,4,8,128]{3,0,2,1:T(8,128)(2,1)S(1)}, bf16[64,4,8,128]{3,0,2,1:T(8,128)(2,1)}, u32[]{:S(2)}) copy-start(bf16[64,4,8,128]{3,0,2,1:T(8,128)(2,1)} %get-tuple-element.34) | copy-start | bytes 1572868
  76.6 22.3 %copy-start.16 = (bf16[64,4,8,128]{3,0,2,1:T(8,128)(2,1)S(1)}, bf16[64,4,8,128]{3,0,2,1:T(8,128)(2,1)}, u32[]{:S(2)}) copy-start(bf16[64,4,8,128]{3,0,2,1:T(8,128)(2,1)} %get-tuple-element.35) | copy-start | bytes 1572868
  86.4 327.9 %copy-start = (bf16[64,4,8,128]{3,0,2,1:T(8,128)(2,1)}, bf16[64,4,8,128]{3,0,2,1:T(8,128)(2,1)S(1)}, u32[]{:S(2)}) copy-start(bf16[64,4,8,128]{3,0,2,1:T(8,128)(2,1)S(1)} %all_gather.3) | copy-start | bytes 1572868
  87.5 322.5 %collective-permute-start.6 = (bf16[16,4,1,128]{3,0,2,1:T(8,128)(2,1)S(1)}, bf16[16,4,1,128]{3,0,2,1:T(8,128)(2,1)S(1)}, u32[]{:S(2)}, u32[]{:S(2)}) collective-permute-start(bf16[16,4,1,128]{3,0,2,1:T(8,128)(2,1)S(1)} %get-tuple-element.48), channel_id=1, source_target_pairs={{0,4},{4,8},{8,12},{12,16},{16,20},{20,24},{24,28},{28,32},{32,36}... | collective-permute-start | bytes 49160 | tf_op jit(solution)/shard_map/ppermute | solution.py:14
  91.0 319.0 %collective-permute-start.7 = (bf16[16,4,1,128]{3,0,2,1:T(8,128)(2,1)S(1)}, bf16[16,4,1,128]{3,0,2,1:T(8,128)(2,1)S(1)}, u32[]{:S(2)}, u32[]{:S(2)}) collective-permute-start(bf16[16,4,1,128]{3,0,2,1:T(8,128)(2,1)S(1)} %get-tuple-element.49), channel_id=1, source_target_pairs={{4,0},{8,4},{12,8},{16,12},{20,16},{24,20},{28,24},{32,28},{36,32}... | collective-permute-start | bytes 49160 | tf_op jit(solution)/shard_map/ppermute | solution.py:17
  92.3 321.9 %collective-permute-start.2 = (bf16[64,4,2,128]{3,0,2,1:T(8,128)(2,1)S(1)}, bf16[64,4,2,128]{3,0,2,1:T(8,128)(2,1)S(1)}, u32[]{:S(2)}, u32[]{:S(2)}) collective-permute-start(bf16[64,4,2,128]{3,0,2,1:T(8,128)(2,1)S(1)} %get-tuple-element.40), channel_id=1, source_target_pairs={{0,4},{4,8},{8,12},{12,16},{16,20},{20,24},{24,28},{28,32},{32,36}... | collective-permute-start | bytes 393224 | tf_op jit(solution)/shard_map/ppermute | solution.py:14
  96.8 317.4 %collective-permute-start.3 = (bf16[64,4,2,128]{3,0,2,1:T(8,128)(2,1)S(1)}, bf16[64,4,2,128]{3,0,2,1:T(8,128)(2,1)S(1)}, u32[]{:S(2)}, u32[]{:S(2)}) collective-permute-start(bf16[64,4,2,128]{3,0,2,1:T(8,128)(2,1)S(1)} %get-tuple-element.41), channel_id=1, source_target_pairs={{4,0},{8,4},{12,8},{16,12},{20,16},{24,20},{28,24},{32,28},{36,32}... | collective-permute-start | bytes 393224 | tf_op jit(solution)/shard_map/ppermute | solution.py:17
  414.2 586.9 %all-reduce.6.cloned.1.call-start = ((), (), s32[]{:S(2)}) async-start(), calls=%async_computation.4 | async-start | bytes 442368 | tf_op jit(solution)/shard_map/psum | solution.py:97
  414.3 3.8 copy-start.1
  414.6 5.6 copy-start.22
  438.7 2.8 copy-start.21
  455.1 2.4 copy-start.3
  455.2 2.4 copy-start.4
  455.2 2.4 copy-start.5
  455.2 2.4 copy-start.6
  455.2 2.4 copy-start.7
  455.2 2.4 copy-start.10
  455.2 2.5 copy-start.11
  455.2 2.5 copy-start.12
  455.2 2.6 copy-start.13
  455.3 2.7 copy-start.14
  (3 other events, 7.0 us)
Sparse Core Ops, SparseCore 0:
  34.9 40.2 reduce-scatter.2
  414.3 27.4 reduce-scatter.4
  455.3 545.7 all-reduce.5
where the time goes:
time: 1010 us
  waiting for transfers between devices  575 us (57%)
  blocking collectives  319 us (32%)
  matrix products  60 us (6%)
  starting transfers between devices  21.7 us (2%)
  between operations  14.6 us (1%)
  local copies, waits for them, and re-layouts  13 us (1%)
    psum x1, waiting for transfers between devices, per_device(): lax.psum((first_local * factor, second_local * factor), 'blocks')  540 us
    psum x1, blocking collectives, per_device(): lax.psum((first_local * factor, second_local * factor), 'blocks')  310 us
    dot_general x72, matrix products, correlate(): jnp.einsum('oi,izyx->ozyx', kernel[a, b, c], window, preferred_element_ty...  50.8 us
    reduce_scatter x1, waiting for transfers between devices, per_device(): lax.psum_scatter(partial_hidden, 'filt', scatter_dimension=0, tiled=True)  35.5 us
  transfers between devices with their start and end apart: 11, of which 2 were waited for; matrix products, arithmetic and copies ran while one was open for 7% of the time, Pallas kernels for 0%

commit v1 on v0

v1 whole, which is shorter than its diff:
```python
import jax
import jax.numpy as jnp
from jax import lax
from jax.experimental import pallas as pl
from jax.experimental.pallas import tpu as pltpu
from jax.sharding import Mesh, PartitionSpec as P

BLOCKS = ("x_lo", "y", "z")
FILT = ("x_hi", "core")
SPLIT = {"x_lo": 2, "y": 4, "z": 8, "x_hi": 2, "core": 2}
BF = jnp.bfloat16
F32 = jnp.float32
SWAP = [(0, 1), (1, 0)]


def dot(left, right):
    return lax.dot_general(left, right, (((1,), (0,)), ((), ())), preferred_element_type=F32)


def dot_cells(left, right):
    return lax.dot_general(left, right, (((1,), (1,)), ((), ())), preferred_element_type=F32)


def shifted(value, amount):
    lane = lax.broadcasted_iota(jnp.int32, value.shape, 1)
    width = value.shape[1]
    moved = pltpu.roll(value, amount % width, 1)
    inside = lane >= amount if amount > 0 else lane < width + amount
    return jnp.where(inside, moved, 0.0)


def forward_kernel(place, vol, vol_lo, vol_hi, w1, w2, cot, out, slope, grads, hidden):
    def row(z, y):
        if y < 0:
            return vol_lo[z, y + 3]
        return vol_hi[z, y - 8] if y >= 8 else vol[z, y]

    weights = w1[...]
    for z in range(4):
        for base in range(-2, 10, 4):
            ys = range(base, base + 4)
            cells = jnp.concatenate(
                [jnp.concatenate([row(z, y - 1), row(z, y), row(z, y + 1)], 0) for y in ys], 1
            )
            product = dot(weights, cells)
            for n, y in enumerate(ys):
                part = product[:, n * 128 : n * 128 + 128]
                pre = shifted(part[:64], 1) + part[64:128] + shifted(part[128:], -1)
                sigma = 1.0 / (1.0 + jnp.exp(-pre))
                value = pre * sigma
                if y < 0:
                    value = jnp.where(place[0] > 0, 0.0, value)
                if y >= 8:
                    value = jnp.where(place[1] > 0, 0.0, value)
                hidden[z, y + 2] = value.astype(BF)
                if -1 <= y <= 8:
                    slope[z, y + 1] = sigma * (1.0 + pre * (1.0 - sigma))
    weights = w2[...]
    total = None
    for p in range(2):
        for base in range(0, 8, 4):
            ys = range(base, base + 4)
            cells = jnp.concatenate(
                [
                    jnp.concatenate(
                        [hidden[p + 2 * q, y + 2 * b] for q in range(2) for b in range(3)], 0
                    )
                    for y in ys
                ],
                1,
            )
            product = dot(weights, cells)
            for n, y in enumerate(ys):
                part = product[:, n * 128 : n * 128 + 128]
                for q in range(2):
                    k = 48 * q
                    value = (
                        shifted(part[k : k + 16], 2)
                        + part[k + 16 : k + 32]
                        + shifted(part[k + 32 : k + 48], -2)
                    )
                    out[p + 2 * q, y] = value.astype(BF)
            left = []
            for y in ys:
                pieces = []
                for q in range(2):
                    own = cot[p + 2 * q, y]
                    wide = own.astype(F32)
                    pieces += [shifted(wide, -2).astype(BF), own, shifted(wide, 2).astype(BF)]
                left.append(jnp.concatenate(pieces, 0))
            term = dot_cells(jnp.concatenate(left, 1), cells)
            total = term if total is None else total + term
    grads[...] = total


def backward_kernel(
    place, cot, cot_lo, cot_hi, slope, vol, vol_lo, vol_hi, w1, w2, second, out, packed, pre_grad
):
    def grad_row(r, z, y):
        if y < 0:
            return cot_lo[r, z, y + 3]
        return cot_hi[r, z, y - 8] if y >= 8 else cot[r, z, y]

    def row(z, y):
        if y < 0:
            return vol_lo[z, y + 3]
        return vol_hi[z, y - 8] if y >= 8 else vol[z, y]

    weights = w2[...]
    for p in range(2):
        for base in range(-1, 9, 2):
            ys = range(base, base + 2)
            cells = jnp.concatenate(
                [
                    jnp.concatenate(
                        [
                            grad_row(r, p + 2 * q, y - 2 * (b - 1))
                            for q in range(2)
                            for b in range(3)
                            for r in range(4)
                        ],
                        0,
                    )
                    for y in ys
                ],
                1,
            )
            product = dot(weights, cells)
            for n, y in enumerate(ys):
                part = product[:, n * 128 : n * 128 + 128]
                for q in range(2):
                    k = 192 * q
                    value = (
                        shifted(part[k : k + 64], -2)
                        + part[k + 64 : k + 128]
                        + shifted(part[k + 128 : k + 192], 2)
                    )
                    value = value * slope[p + 2 * q, y + 1]
                    if y < 0:
                        value = jnp.where(place[0] > 0, 0.0, value)
                    if y >= 8:
                        value = jnp.where(place[1] > 0, 0.0, value)
                    pre_grad[p + 2 * q, y + 1] = value.astype(BF)
    weights = w1[...]
    mine = pl.multiple_of(place[2] * 16, 16)
    total = None
    for z in range(4):
        for base in range(0, 8, 4):
            ys = range(base, base + 4)
            cells = jnp.concatenate(
                [
                    jnp.concatenate([pre_grad[z, y + 1 - (b - 1)] for b in range(3)], 0)
                    for y in ys
                ],
                1,
            )
            product = dot(weights, cells)
            for n, y in enumerate(ys):
                part = product[:, n * 128 : n * 128 + 128]
                value = shifted(part[:16], -1) + part[16:32] + shifted(part[32:48], 1)
                out[z, y] = value.astype(BF)
            left = []
            for y in ys:
                own = pre_grad[z, y + 1, pl.ds(mine, 16), :]
                wide = own.astype(F32)
                left.append(
                    jnp.concatenate([shifted(wide, -1).astype(BF), own, shifted(wide, 1).astype(BF)], 0)
                )
            source = jnp.concatenate(
                [jnp.concatenate([row(z, y - 1), row(z, y), row(z, y + 1)], 0) for y in ys], 1
            )
            term = dot_cells(jnp.concatenate(left, 1), source)
            total = term if total is None else total + term
    raw = second[...]
    rows = jnp.concatenate(
        [
            raw[48:, :192],
            raw[:48, :192] + raw[48:, 192:],
            raw[:48, 192:],
            total,
        ],
        0,
    ) * (1.0 / 512.0)
    for k in range(24):
        packed[k] = rows[8 * k : 8 * k + 8, :128]
    for k in range(12):
        packed[24 + k] = jnp.concatenate(
            [rows[8 * k : 8 * k + 8, 128:], rows[96 + 8 * k : 104 + 8 * k, 128:]], 1
        )
    packed[36:] = jnp.zeros((28, 8, 128), F32)


def spread_kernel(tiles, first, second):
    for g in range(4):
        for c in range(3):
            for half in range(2):
                t = g * 6 + c * 2 + half
                main = tiles[t]
                rest = tiles[24 + t % 12]
                parts = [main[:, :64], main[:, 64:], rest[:, :64] if t < 12 else rest[:, 64:]]
                for b in range(3):
                    if g < 3:
                        second[g, b, c, 8 * half : 8 * half + 8, :] = parts[b]
                    else:
                        first[b, c, 8 * half : 8 * half + 8, :] = parts[b]


SMEM = pl.BlockSpec(memory_space=pltpu.SMEM)
VMEM = pl.BlockSpec(memory_space=pltpu.VMEM)


def call(kernel, operands, outs, scratch=(), scalars=True):
    specs = [SMEM] + [VMEM] * (len(operands) - 1) if scalars else [VMEM] * len(operands)
    return pl.pallas_call(
        kernel,
        in_specs=specs,
        out_specs=tuple(VMEM for _ in outs),
        out_shape=tuple(jax.ShapeDtypeStruct(shape, kind) for shape, kind in outs),
        scratch_shapes=list(scratch),
    )(*operands)


def neighbours(rows):
    count = 64
    forward = [(i, i + 1) for i in range(count - 1)]
    backward = [(i + 1, i) for i in range(count - 1)]
    return (
        lax.ppermute(rows[..., 5:8, :, :], BLOCKS, forward),
        lax.ppermute(rows[..., 0:3, :, :], BLOCKS, backward),
    )


def per_device(volume, w_first, w_second, cotangent):
    block = lax.axis_index(BLOCKS)
    mine = lax.axis_index(FILT)
    place = jnp.stack([block == 0, block == 63, mine]).astype(jnp.int32)
    vol = volume.transpose(1, 2, 0, 3)
    vol_lo, vol_hi = neighbours(vol)
    cot = cotangent.transpose(1, 2, 0, 3)
    kernels = jnp.concatenate([w_first.reshape(9, 16, 64), w_second.reshape(27, 16, 64)], 0)
    bundle = jnp.concatenate(
        [cot.reshape(32, 16, 128), jnp.concatenate([kernels[:18], kernels[18:]], 2)], 0
    )[None]
    bundle = jnp.concatenate([bundle, lax.ppermute(bundle, "x_hi", SWAP)], 0)
    bundle = jnp.concatenate([bundle, lax.ppermute(bundle, "core", SWAP)], 0)
    cot_all = bundle[:, :32].reshape(4, 4, 8, 16, 128)
    cot_lo, cot_hi = neighbours(cot_all)
    kernels = jnp.concatenate([bundle[:, 32:, :, :64], bundle[:, 32:, :, 64:]], 1)
    places = [((f ^ mine) & 1) * 2 + ((f ^ mine) >> 1) for f in range(4)]
    ordered = jnp.stack(
        [lax.dynamic_index_in_dim(kernels[:, :9], at, 0, False) for at in places]
    )
    full_first = ordered.reshape(4, 3, 3, 16, 64)
    w1_forward = full_first.transpose(2, 0, 3, 1, 4).reshape(192, 192)
    own_inputs = lax.dynamic_slice_in_dim(full_first, mine * 16, 16, 4)
    w1_backward = own_inputs.transpose(2, 4, 1, 0, 3).reshape(48, 192)
    w2_forward = (
        jnp.stack([jnp.stack([w_second[1 + q - z] for q in range(2)]) for z in range(2)])
        .transpose(0, 3, 4, 1, 2, 5)
        .reshape(96, 384)
    )
    full_second = kernels[:, 9:].reshape(4, 3, 3, 3, 16, 64)
    w2_backward = (
        jnp.stack([jnp.stack([full_second[:, 1 + z - q] for q in range(2)]) for z in range(2)])
        .transpose(0, 4, 6, 1, 3, 2, 5)
        .reshape(384, 384)
    )
    output, slope, second = call(
        forward_kernel,
        (place, vol, vol_lo, vol_hi, w1_forward, w2_forward, cot),
        (((4, 8, 16, 128), BF), ((4, 10, 64, 128), F32), ((96, 384), F32)),
        [pltpu.VMEM((4, 12, 64, 128), BF)],
    )
    input_grad, packed = call(
        backward_kernel,
        (place, cot_all, cot_lo, cot_hi, slope, vol, vol_lo, vol_hi, w1_backward, w2_backward, second),
        (((4, 8, 16, 128), BF), ((64, 8, 128), F32)),
        [pltpu.VMEM((4, 10, 64, 128), BF)],
    )
    shares = lax.all_to_all(packed, BLOCKS, 0, 0)
    summed = jnp.broadcast_to(jnp.sum(shares, 0)[None], (64, 8, 128))
    tiles = lax.all_to_all(summed, BLOCKS, 0, 0)
    first_grad, second_grad = call(
        spread_kernel,
        (tiles,),
        (((3, 3, 16, 64), F32), ((3, 3, 3, 16, 64), F32)),
        scalars=False,
    )
    return (output.transpose(2, 0, 1, 3), input_grad.transpose(2, 0, 1, 3), first_grad, second_grad)


def solution(mesh):
    fine = Mesh(mesh.devices.reshape(tuple(SPLIT.values())), tuple(SPLIT))
    return jax.shard_map(
        per_device,
        mesh=fine,
        in_specs=(
            P(None, None, BLOCKS, None),
            P(None, None, FILT, None),
            P(None, None, None, FILT, None),
            P(FILT, None, BLOCKS, None),
        ),
        out_specs=(
            P(FILT, None, BLOCKS, None),
            P(FILT, None, BLOCKS, None),
            P(None, None, FILT, None),
            P(None, None, None, FILT, None),
        ),
        check_vma=False,
    )
```

time: 1010 us -> 94.2 us (0.09)
  waiting for transfers between devices: 575 us -> 17.2 us
  blocking collectives: 319 us -> 32.3 us
  matrix products: 60 us -> 0 us
  between operations: 14.6 us -> 0.95 us
  Pallas kernels: 0 us -> 10.8 us
    psum x1 -> x0, waiting for transfers between devices: 540 us -> none  [per_device(): lax.psum((first_local * factor, second_local * factor), 'blocks')]
    psum x1 -> x0, blocking collectives: 310 us -> none  [per_device(): lax.psum((first_local * factor, second_local * factor), 'blocks')]
    dot_general x108 -> x0, matrix products: 60 us -> none  [the longest x72 50.8 us: correlate(): jnp.einsum('oi,izyx->ozyx', kernel[a, b, c], window, preferred_element_ty...]
    reduce_scatter x2 -> x0, waiting for transfers between devices: 35.5 us -> none  [the longest x1 35.5 us: per_device(): lax.psum_scatter(partial_hidden, 'filt', scatter_dimension=0, tiled=True)]
    all_to_all x0 -> x1, blocking collectives: none -> 32.3 us  [per_device(): shares = lax.all_to_all(packed, BLOCKS, 0, 0)]
    all_to_all x0 -> x1, waiting for transfers between devices: none -> 11.3 us  [per_device(): tiles = lax.all_to_all(summed, BLOCKS, 0, 0)]
    pallas_call x0 -> x3, Pallas kernels: none -> 10.8 us  [call(): pl.pallas_call(kernel, in_specs=specs, out_specs=tuple((VMEM for _ in out...]
    ppermute x8 -> x6, starting transfers between devices: 21.5 us -> 14.1 us  [the longest x2 9.12 us: neighbours(): lax.ppermute(rows[..., 5:8, :, :], BLOCKS, forward)]
  transfers between devices with their start and end apart: 11 -> 7, of which waited for: 2 -> 2; matrix products, arithmetic and copies ran while one was open for 7% -> 8% of each run, Pallas kernels for 0% -> 4%
where the time goes in v1:
time: 94.2 us; the launch traced here: 93.5 us
  blocking collectives  32.3 us (34%)
  starting transfers between devices  18.7 us (20%)
  waiting for transfers between devices  17.2 us (18%)
  local copies, waits for them, and re-layouts  11.5 us (12%)
  Pallas kernels  10.8 us (11%)
  other arithmetic  2.15 us (2%)
  between operations  0.95 us (1%)
    all_to_all x1, blocking collectives, per_device(): shares = lax.all_to_all(packed, BLOCKS, 0, 0)  32.3 us
    all_to_all x1, waiting for transfers between devices, per_device(): tiles = lax.all_to_all(summed, BLOCKS, 0, 0)  11.3 us
    pallas_call x3, Pallas kernels, call(): pl.pallas_call(kernel, in_specs=specs, out_specs=tuple((VMEM for _ in out...  10.8 us
    ppermute x2, starting transfers between devices, neighbours(): lax.ppermute(rows[..., 5:8, :, :], BLOCKS, forward)  9.12 us
    ppermute x1, waiting for transfers between devices, per_device(): bundle = jnp.concatenate([bundle, lax.ppermute(bundle, 'x_hi', SWAP)], 0)  5.89 us
    unnamed x26, local copies, waits for them, and re-layouts  4.78 us
    all_to_all x1, starting transfers between devices, per_device(): tiles = lax.all_to_all(summed, BLOCKS, 0, 0)  4.62 us
    ppermute x2, starting transfers between devices, neighbours(): lax.ppermute(rows[..., 0:3, :, :], BLOCKS, backward)  2.58 us
  transfers between devices with their start and end apart: 7, of which 2 were waited for; matrix products, arithmetic and copies ran while one was open for 8% of the time, Pallas kernels for 4%

profile of v1, /device:TPU:4, one launch (start us, length us, event | category | flops | bytes accessed | tf_op | source)
XLA Modules:
  0.0 93.5 jit_solution(13156800377345542055)
XLA Ops:
  0.6 1.0 %copy.32 = bf16[16,4,8,128]{3,0,2,1:T(8,128)(2,1)S(1)} copy(bf16[16,4,8,128]{3,2,1,0:T(8,128)(2,1)} %param.7) | data formatting | bytes 262144 | tf_op args[3]
  1.7 1.0 %slice_bitcast_fusion.4 = (bf16[1,2,3,3,16,64]{5,4,3,2,1,0:T(8,128)(2,1)S(1)}, bf16[1,2,3,3,16,64]{5,4,3,2,1,0:T(8,128)(2,1)S(1)}, bf16[2,3,3,16,64]{4,3,2,1,0:T(8,128)(2,1)S(1)}) fusion(bf16[3,3,3,16,64]{4,3,2,1,0:T(8,128)(2,1)} %param.6), kind=kLoop, calls=%fused_computation.24 | loop fusion | bytes 184320 | tf_op jit(solution)/shard_map/stack | solution.py:258
  2.7 0.9 fusion.2
  3.6 2.3 %collective-permute-start.2 = (bf16[1,50,16,128]{3,2,1,0:T(8,128)(2,1)S(1)}, bf16[1,50,16,128]{3,2,1,0:T(8,128)(2,1)S(1)}, u32[]{:S(2)}, u32[]{:S(2)}) collective-permute-start(bf16[1,50,16,128]{3,2,1,0:T(8,128)(2,1)S(1)} %fusion.2), channel_id=1, source_target_pairs={{0,2},{2,0},{1,3},{3,1},{4,6},{6,4},{5,7},{7,5},{8,10},{10,8},{9,1... | collective-permute-start | bytes 614408 | tf_op jit(solution)/shard_map/ppermute | solution.py:244
  5.9 0.2 copy.31
  6.1 5.9 %collective-permute-done.2 = bf16[1,50,16,128]{3,2,1,0:T(8,128)(2,1)S(1)} collective-permute-done((bf16[1,50,16,128]{3,2,1,0:T(8,128)(2,1)S(1)}, bf16[1,50,16,128]{3,2,1,0:T(8,128)(2,1)S(1)}, u32[]{:S(2)}, u32[]{:S(2)}) %collective-permute-start.2) | collective-permute-done | bytes 204832 | tf_op jit(solution)/shard_map/ppermute | solution.py:244
  12.2 1.3 %collective-permute-start.1 = (bf16[4,3,64,128]{3,2,1,0:T(8,128)(2,1)S(1)}, bf16[4,3,64,128]{3,2,1,0:T(8,128)(2,1)S(1)}, u32[]{:S(2)}, u32[]{:S(2)}) collective-permute-start(bf16[4,3,64,128]{3,2,1,0:T(8,128)(2,1)S(1)} %get-tuple-element.30), channel_id=1, source_target_pairs={{4,0},{8,4},{12,8},{16,12},{20,16},{24,20},{28,24},{32,28},{36,32}... | collective-permute-start | bytes 589832 | tf_op jit(solution)/shard_map/ppermute | solution.py:229
  13.5 4.6 %collective-permute-start = (bf16[4,3,64,128]{3,2,1,0:T(8,128)(2,1)S(1)}, bf16[4,3,64,128]{3,2,1,0:T(8,128)(2,1)S(1)}, u32[]{:S(2)}, u32[]{:S(2)}) collective-permute-start(bf16[4,3,64,128]{3,2,1,0:T(8,128)(2,1)S(1)} %get-tuple-element.31), channel_id=1, source_target_pairs={{0,4},{4,8},{8,12},{12,16},{16,20},{20,24},{24,28},{28,32},{32,36}... | collective-permute-start | bytes 589832 | tf_op jit(solution)/shard_map/ppermute | solution.py:228
  18.2 0.8 reshape.45.w2
  19.0 0.6 pad_add_fusion.place
  19.8 0.1 fusion.3
  20.2 0.1 copy.19
  20.3 0.7 reshape.47.w1
  21.2 0.8 reshape.44.w1
  22.1 1.3 %collective-permute-start.5 = (bf16[4,4,3,16,128]{4,3,2,1,0:T(8,128)(2,1)S(1)}, bf16[4,4,3,16,128]{4,3,2,1,0:T(8,128)(2,1)S(1)}, u32[]{:S(2)}, u32[]{:S(2)}) collective-permute-start(bf16[4,4,3,16,128]{4,3,2,1,0:T(8,128)(2,1)S(1)} %get-tuple-element.28), channel_id=1, source_target_pairs={{4,0},{8,4},{12,8},{16,12},{20,16},{24,20},{28,24},{32,28},{36,32}... | collective-permute-start | bytes 589832 | tf_op jit(solution)/shard_map/ppermute | solution.py:229
  23.4 4.6 %collective-permute-start.4 = (bf16[4,4,3,16,128]{4,3,2,1,0:T(8,128)(2,1)S(1)}, bf16[4,4,3,16,128]{4,3,2,1,0:T(8,128)(2,1)S(1)}, u32[]{:S(2)}, u32[]{:S(2)}) collective-permute-start(bf16[4,4,3,16,128]{4,3,2,1,0:T(8,128)(2,1)S(1)} %get-tuple-element.29), channel_id=1, source_target_pairs={{0,4},{4,8},{8,12},{12,16},{16,20},{20,24},{24,28},{28,32},{32,36}... | collective-permute-start | bytes 589832 | tf_op jit(solution)/shard_map/ppermute | solution.py:228
  28.1 0.1 maximum_bitcast_fusion
  28.3 0.4 copy.22
  28.7 0.6 reshape.49
  29.2 0.9 copy.23.w2
  30.2 0.7 copy-done.4
  30.9 3.7 %shard_map.75 = (bf16[4,8,16,128]{3,2,1,0:T(8,128)(2,1)}, f32[4,10,64,128]{3,2,1,0:T(8,128)}, f32[96,384]{1,0:T(8,128)}) custom-call(s32[3]{0:T(128)} %pad_add_fusion.place, bf16[4,8,64,128]{3,2,1,0:T(8,128)(2,1)} %bitcast.50, bf16[4,3,64,128]{3,2,1,0:T(8,128)(2,1)} %copy-done.5, bf16[4,3,64,128]{3,2,1,0:T(8,128)(2,1)} %copy-done.4, ...), custom_call_target="tpu_custom_call" | custom-call | tf_op jit(solution)/shard_map/pallas_call | solution.py:214
  34.7 0.6 copy-done.7
  35.4 5.3 %shard_map.76 = (bf16[4,8,16,128]{3,2,1,0:T(8,128)(2,1)}, f32[64,8,128]{2,1,0:T(8,128)}) custom-call(s32[3]{0:T(128)} %pad_add_fusion.place, bf16[4,4,8,16,128]{4,3,2,1,0:T(8,128)(2,1)} %bitcast.53, bf16[4,4,3,16,128]{4,3,2,1,0:T(8,128)(2,1)} %copy-done.8, bf16[4,4,3,16,128]{4,3,2,1,0:T(8,128)(2,1)} %copy-done.7, ...), custom_call_target="tpu_custom_call" | custom-call | tf_op jit(solution)/shard_map/pallas_call | solution.py:214
  40.7 32.3 %all_to_all.10 = f32[64,8,128]{2,1,0:T(8,128)S(1)} all-to-all(f32[64,8,128]{2,1,0:T(8,128)} %get-tuple-element.15), channel_id=1, replica_groups=mesh['x_lo'=2,'y'=4,'z'=8,'x_hi'=2,'core'=2] {'x_lo','y','z'}, dimensions={0} | all-to-all | bytes 524288 | tf_op jit(solution)/shard_map/all_to_all | solution.py:280
  73.0 0.7 broadcast_in_dim.10
  73.7 4.6 %all-to-all-start.1 = ((f32[64,8,128]{2,1,0:T(8,128)}), f32[64,8,128]{2,1,0:T(8,128)S(1)}, u32[]{:S(2)}, u32[]{:S(2)}) async-start(f32[64,8,128]{2,1,0:T(8,128)} %broadcast_in_dim.10), calls=%async_computation.1 | async-start | bytes 524288 | tf_op jit(solution)/shard_map/all_to_all | solution.py:282
  78.4 0.7 copy.24
  79.1 0.7 copy.25
  79.8 11.3 %all-to-all-done.1.tiles = f32[64,8,128]{2,1,0:T(8,128)S(1)} async-done(((f32[64,8,128]{2,1,0:T(8,128)}), f32[64,8,128]{2,1,0:T(8,128)S(1)}, u32[]{:S(2)}, u32[]{:S(2)}) %all-to-all-start.1) | async-done | bytes 262176 | tf_op jit(solution)/shard_map/all_to_all | solution.py:282
  91.1 0.7 copy-done.3
  91.8 1.7 %shard_map.77 = (f32[3,3,16,64]{3,2,1,0:T(8,128)}, f32[3,3,3,16,64]{4,3,2,1,0:T(8,128)}) custom-call(f32[64,8,128]{2,1,0:T(8,128)} %copy-done.3), custom_call_target="tpu_custom_call" | custom-call | tf_op jit(solution)/shard_map/pallas_call | solution.py:214
  (41 shorter events, 1.2 us)
Async XLA Ops:
  0.6 5.2 %copy-start.6 = (bf16[64,4,8,128]{3,2,1,0:T(8,128)(2,1)S(1)}, bf16[64,4,8,128]{3,2,1,0:T(8,128)(2,1)}, u32[]{:S(2)}) copy-start(bf16[64,4,8,128]{3,2,1,0:T(8,128)(2,1)} %param.4) | copy-start | bytes 1572868
  1.7 10.4 %copy-start.2 = (bf16[16,4,8,128]{3,0,2,1:T(8,128)(2,1)}, bf16[16,4,8,128]{3,0,2,1:T(8,128)(2,1)S(1)}, u32[]{:S(2)}) copy-start(bf16[16,4,8,128]{3,0,2,1:T(8,128)(2,1)S(1)} %copy.32) | copy-start | bytes 393220
  3.6 8.4 %collective-permute-start.2 = (bf16[1,50,16,128]{3,2,1,0:T(8,128)(2,1)S(1)}, bf16[1,50,16,128]{3,2,1,0:T(8,128)(2,1)S(1)}, u32[]{:S(2)}, u32[]{:S(2)}) collective-permute-start(bf16[1,50,16,128]{3,2,1,0:T(8,128)(2,1)S(1)} %fusion.2), channel_id=1, source_target_pairs={{0,2},{2,0},{1,3},{3,1},{4,6},{6,4},{5,7},{7,5},{8,10},{10,8},{9,1... | collective-permute-start | bytes 614408 | tf_op jit(solution)/shard_map/ppermute | solution.py:244
  6.1 13.0 %copy-start = (bf16[64,4,8,128]{3,0,2,1:T(8,128)(2,1)}, bf16[64,4,8,128]{3,0,2,1:T(8,128)(2,1)S(1)}, u32[]{:S(2)}) copy-start(bf16[64,4,8,128]{3,0,2,1:T(8,128)(2,1)S(1)} %copy.31) | copy-start | bytes 1572868
  12.0 7.6 %collective-permute-start.3 = (bf16[2,50,16,128]{3,2,1,0:T(8,128)(2,1)S(1)}, bf16[2,50,16,128]{3,2,1,0:T(8,128)(2,1)S(1)}, u32[]{:S(2)}, u32[]{:S(2)}) collective-permute-start(bf16[2,50,16,128]{3,2,1,0:T(8,128)(2,1)S(1)} %pad_maximum_fusion.2), channel_id=1, source_target_pairs={{0,1},{1,0},{2,3},{3,2},{4,5},{5,4},{6,7},{7,6},{8,9},{9,8},{10,11... | collective-permute-start | bytes 1228808 | tf_op jit(solution)/shard_map/ppermute | solution.py:245
  12.2 18.0 %collective-permute-start.1 = (bf16[4,3,64,128]{3,2,1,0:T(8,128)(2,1)S(1)}, bf16[4,3,64,128]{3,2,1,0:T(8,128)(2,1)S(1)}, u32[]{:S(2)}, u32[]{:S(2)}) collective-permute-start(bf16[4,3,64,128]{3,2,1,0:T(8,128)(2,1)S(1)} %get-tuple-element.30), channel_id=1, source_target_pairs={{4,0},{8,4},{12,8},{16,12},{20,16},{24,20},{28,24},{32,28},{36,32}... | collective-permute-start | bytes 589832 | tf_op jit(solution)/shard_map/ppermute | solution.py:229
  13.5 16.7 %collective-permute-start = (bf16[4,3,64,128]{3,2,1,0:T(8,128)(2,1)S(1)}, bf16[4,3,64,128]{3,2,1,0:T(8,128)(2,1)S(1)}, u32[]{:S(2)}, u32[]{:S(2)}) collective-permute-start(bf16[4,3,64,128]{3,2,1,0:T(8,128)(2,1)S(1)} %get-tuple-element.31), channel_id=1, source_target_pairs={{0,4},{4,8},{8,12},{12,16},{16,20},{20,24},{24,28},{28,32},{32,36}... | collective-permute-start | bytes 589832 | tf_op jit(solution)/shard_map/ppermute | solution.py:228
  19.8 2.3 %copy-start.1 = (bf16[4,32,16,128]{3,2,1,0:T(8,128)(2,1)}, bf16[4,32,16,128]{3,2,1,0:T(8,128)(2,1)S(1)}, u32[]{:S(2)}) copy-start(bf16[4,32,16,128]{3,2,1,0:T(8,128)(2,1)S(1)} %slice.73) | copy-start | bytes 1572868
  22.1 12.5 %collective-permute-start.5 = (bf16[4,4,3,16,128]{4,3,2,1,0:T(8,128)(2,1)S(1)}, bf16[4,4,3,16,128]{4,3,2,1,0:T(8,128)(2,1)S(1)}, u32[]{:S(2)}, u32[]{:S(2)}) collective-permute-start(bf16[4,4,3,16,128]{4,3,2,1,0:T(8,128)(2,1)S(1)} %get-tuple-element.28), channel_id=1, source_target_pairs={{4,0},{8,4},{12,8},{16,12},{20,16},{24,20},{28,24},{32,28},{36,32}... | collective-permute-start | bytes 589832 | tf_op jit(solution)/shard_map/ppermute | solution.py:229
  23.4 11.2 %collective-permute-start.4 = (bf16[4,4,3,16,128]{4,3,2,1,0:T(8,128)(2,1)S(1)}, bf16[4,4,3,16,128]{4,3,2,1,0:T(8,128)(2,1)S(1)}, u32[]{:S(2)}, u32[]{:S(2)}) collective-permute-start(bf16[4,4,3,16,128]{4,3,2,1,0:T(8,128)(2,1)S(1)} %get-tuple-element.29), channel_id=1, source_target_pairs={{0,4},{4,8},{8,12},{12,16},{16,20},{20,24},{24,28},{28,32},{32,36}... | collective-permute-start | bytes 589832 | tf_op jit(solution)/shard_map/ppermute | solution.py:228
  30.2 0.7 copy-start.4
  30.2 0.7 copy-start.5
  34.6 0.7 copy-start.7
  34.6 0.7 copy-start.8
  40.7 37.7 %copy-start.9 = (bf16[4,8,16,128]{3,2,1,0:T(8,128)(2,1)S(1)}, bf16[4,8,16,128]{3,2,1,0:T(8,128)(2,1)}, u32[]{:S(2)}) copy-start(bf16[4,8,16,128]{3,2,1,0:T(8,128)(2,1)} %get-tuple-element.11) | copy-start | bytes 393220
  40.7 38.4 %copy-start.10 = (bf16[4,8,16,128]{3,2,1,0:T(8,128)(2,1)S(1)}, bf16[4,8,16,128]{3,2,1,0:T(8,128)(2,1)}, u32[]{:S(2)}) copy-start(bf16[4,8,16,128]{3,2,1,0:T(8,128)(2,1)} %get-tuple-element.14) | copy-start | bytes 393220
  73.7 17.3 %all-to-all-start.1 = ((f32[64,8,128]{2,1,0:T(8,128)}), f32[64,8,128]{2,1,0:T(8,128)S(1)}, u32[]{:S(2)}, u32[]{:S(2)}) async-start(f32[64,8,128]{2,1,0:T(8,128)} %broadcast_in_dim.10), calls=%async_computation.1 | async-start | bytes 524288 | tf_op jit(solution)/shard_map/all_to_all | solution.py:282
  91.1 0.7 copy-start.3

commit v2 on v1

v2 whole, which is shorter than its diff:
```python
import jax
import jax.numpy as jnp
from jax import lax
from jax.experimental import pallas as pl
from jax.experimental.pallas import tpu as pltpu
from jax.sharding import Mesh, PartitionSpec as P


BLOCKS = ("x_lo", "y", "z")
FILT = ("x_hi", "core")
SPLIT = {"x_lo": 2, "y": 4, "z": 8, "x_hi": 2, "core": 2}
BF = jnp.bfloat16
F32 = jnp.float32
SWAP = [(0, 1), (1, 0)]


def dot(left, right):
    return lax.dot_general(left, right, (((1,), (0,)), ((), ())), preferred_element_type=F32)


def dot_cells(left, right):
    return lax.dot_general(left, right, (((1,), (1,)), ((), ())), preferred_element_type=F32)


def shifted(value, amount):
    lane = lax.broadcasted_iota(jnp.int32, value.shape, 1)
    width = value.shape[1]
    moved = pltpu.roll(value, amount % width, 1)
    inside = lane >= amount if amount > 0 else lane < width + amount
    return jnp.where(inside, moved, 0.0)


def prepare_kernel(volume, cotangent, w_first, w_second, vol, down, up, grads, kernels, own):
    for z in range(4):
        rows = jnp.swapaxes(volume[:, z].astype(F32), 0, 1).astype(BF)
        vol[z] = rows
        mine = jnp.swapaxes(cotangent[:, z].astype(F32), 0, 1).astype(BF)
        grads[8 * z : 8 * z + 8] = mine
        own[8 * z : 8 * z + 8] = mine
        for n in range(3):
            k = 3 * z + n
            down[k] = mine[5 + n]
            up[k] = mine[n]
            down[12 + 4 * k : 16 + 4 * k] = rows[5 + n].reshape(4, 16, 128)
            up[12 + 4 * k : 16 + 4 * k] = rows[n].reshape(4, 16, 128)
    strips = [w_first[b, c] for c in range(3) for b in range(3)]
    strips += [w_second[a, b, c] for a in range(3) for b in range(3) for c in range(3)]
    for n in range(18):
        pair = jnp.concatenate(strips[2 * n : 2 * n + 2], 1)
        kernels[n] = pair
        own[32 + n] = pair


def strip(kernels, base, n):
    k = base + 3 * (n // 2)
    if n % 2 == 0:
        return jnp.concatenate([kernels[k], kernels[k + 1][:, :64]], 1)
    return jnp.concatenate([kernels[k + 1][:, 64:], kernels[k + 2]], 1)


def volume_row(vol, low, high, z, y):
    if 0 <= y < 8:
        return vol[z, y]
    source, n = (low, y + 3) if y < 0 else (high, y - 8)
    k = 12 + 4 * (3 * z + n)
    return source[k : k + 4].reshape(64, 128)


def stacked_rows(vol, low, high, z, y):
    return jnp.concatenate([volume_row(vol, low, high, z, y + n) for n in (-1, 0, 1)], 0)


def build_first(spot, kernels, w1_full):
    for r in range(4):
        f = pl.multiple_of((spot ^ r) * 16, 16)
        for c in range(3):
            w1_full[c, pl.ds(f, 16), :] = strip(*kernels[r], c)


def forward_kernel(
    place,
    vol,
    low,
    high,
    part0,
    kernels0,
    kernels1,
    kernels2,
    kernels3,
    hidden,
    slope,
    grads,
    w2_turned,
    w1_full,
):
    kernels = ((kernels0, 0), (kernels1, 32), (kernels2, 0), (kernels3, 0))
    build_first(place[2], kernels, w1_full)

    turned = jnp.concatenate(
        [
            jnp.concatenate([strip(*kernels[r], 3 + 3 * (1 + z - q) + b) for z in range(2)], 1)
            for q in range(2)
            for b in range(3)
            for r in range(4)
        ],
        0,
    )
    w2_turned[...] = turned.T.reshape(6, 64, 384)
    weights = w1_full[...].reshape(192, 192)
    for z in range(4):
        for base in range(-2, 10, 4):
            ys = range(base, base + 4)
            cells = jnp.concatenate([stacked_rows(vol, low, high, z, y) for y in ys], 1)
            product = dot(weights, cells)
            for n, y in enumerate(ys):
                part = product[:, n * 128 : n * 128 + 128]
                pre = shifted(part[:64], 1) + part[64:128] + shifted(part[128:], -1)
                sigma = 1.0 / (1.0 + jnp.exp(-pre))
                value = pre * sigma
                if y < 0:
                    value = jnp.where(place[0] > 0, 0.0, value)
                if y >= 8:
                    value = jnp.where(place[1] > 0, 0.0, value)
                hidden[z, y + 2] = value.astype(BF)
                if -1 <= y <= 8:
                    slope[z, y + 1] = sigma * (1.0 + pre * (1.0 - sigma))
    total = None
    for p in range(2):
        for base in range(0, 8, 4):
            ys = range(base, base + 4)
            left = []
            for y in ys:
                pieces = []
                for q in range(2):
                    own = part0[8 * (p + 2 * q) + y]
                    wide = own.astype(F32)
                    pieces += [shifted(wide, -2).astype(BF), own, shifted(wide, 2).astype(BF)]
                left.append(jnp.concatenate(pieces, 0))
            term = dot_cells(jnp.concatenate(left, 1), hidden_rows(hidden, p, ys))
            total = term if total is None else total + term
    grads[...] = total


def hidden_rows(hidden, p, ys):
    return jnp.concatenate(
        [
            jnp.concatenate([hidden[p + 2 * q, y + 2 * b] for q in range(2) for b in range(3)], 0)
            for y in ys
        ],
        1,
    )


def grad_rows(parts, rims, p, ys):
    def grad_row(r, z, y):
        if 0 <= y < 8:
            return parts[r][8 * z + y]
        return rims[r][3 * z + y + 3] if y < 0 else rims[r][12 + 3 * z + y - 8]

    return jnp.concatenate(
        [
            jnp.concatenate(
                [
                    grad_row(r, p + 2 * q, y - 2 * (b - 1))
                    for q in range(2)
                    for b in range(3)
                    for r in range(4)
                ],
                0,
            )
            for y in ys
        ],
        1,
    )


def first_grad_kernel(
    place,
    vol,
    low,
    high,
    part0,
    part1,
    part2,
    part3,
    rim0,
    rim1,
    rim2,
    rim3,
    slope,
    second,
    w2_turned,
    packed,
    own_grad,
):
    parts = (part0, part1, part2, part3)
    rims = (rim0, rim1, rim2, rim3)
    mine = pl.multiple_of(place[2] * 16, 16)
    weights = w2_turned[:, pl.ds(mine, 16), :].reshape(96, 384)
    for p in range(2):
        for base in range(0, 8, 4):
            ys = range(base, base + 4)
            product = dot(weights, grad_rows(parts, rims, p, ys))
            for n, y in enumerate(ys):
                part = product[:, n * 128 : n * 128 + 128]
                for q in range(2):
                    k = 48 * q
                    value = (
                        shifted(part[k : k + 16], -2)
                        + part[k + 16 : k + 32]
                        + shifted(part[k + 32 : k + 48], 2)
                    )
                    value = value * slope[p + 2 * q, y + 1, pl.ds(mine, 16), :]
                    own_grad[p + 2 * q, y] = value.astype(BF)
    total = None
    for z in range(4):
        for base in range(0, 8, 4):
            ys = range(base, base + 4)
            left = []
            for y in ys:
                own = own_grad[z, y]
                wide = own.astype(F32)
                left.append(
                    jnp.concatenate([shifted(wide, -1).astype(BF), own, shifted(wide, 1).astype(BF)], 0)
                )
            source = jnp.concatenate([stacked_rows(vol, low, high, z, y) for y in ys], 1)
            term = dot_cells(jnp.concatenate(left, 1), source)
            total = term if total is None else total + term
    raw = second[...]
    rows = jnp.concatenate(
        [raw[48:, :192], raw[:48, :192] + raw[48:, 192:], raw[:48, 192:], total], 0
    ) * (1.0 / 512.0)
    for k in range(24):
        packed[k] = rows[8 * k : 8 * k + 8, :128]
    for k in range(12):
        packed[24 + k] = jnp.concatenate(
            [rows[8 * k : 8 * k + 8, 128:], rows[96 + 8 * k : 104 + 8 * k, 128:]], 1
        )
    packed[36:] = jnp.zeros((28, 8, 128), F32)


def outputs_kernel(
    place,
    hidden,
    part0,
    part1,
    part2,
    part3,
    rim0,
    rim1,
    rim2,
    rim3,
    slope,
    kernels0,
    kernels1,
    kernels2,
    kernels3,
    w2_turned,
    out,
    input_grad,
    pre_grad,
    w1_full,
    w1_turned,
):
    kernels = ((kernels0, 0), (kernels1, 32), (kernels2, 0), (kernels3, 0))
    build_first(place[2], kernels, w1_full)
    parts = (part0, part1, part2, part3)
    rims = (rim0, rim1, rim2, rim3)
    mine = pl.multiple_of(place[2] * 16, 16)
    weights = jnp.concatenate(
        [
            jnp.concatenate(
                [
                    strip(kernels0, 0, 3 + 3 * (1 + q - z) + b)[:, 64 * c : 64 * c + 64]
                    for q in range(2)
                    for b in range(3)
                ],
                1,
            )
            for z in range(2)
            for c in range(3)
        ],
        0,
    )
    for p in range(2):
        for base in range(0, 8, 4):
            ys = range(base, base + 4)
            product = dot(weights, hidden_rows(hidden, p, ys))
            for n, y in enumerate(ys):
                part = product[:, n * 128 : n * 128 + 128]
                for q in range(2):
                    k = 48 * q
                    value = (
                        shifted(part[k : k + 16], 2)
                        + part[k + 16 : k + 32]
                        + shifted(part[k + 32 : k + 48], -2)
                    )
                    out[p + 2 * q, y] = value.astype(BF)
    weights = w2_turned[...].reshape(384, 384)
    for p in range(2):
        for base in range(-1, 9, 2):
            ys = range(base, base + 2)
            product = dot(weights, grad_rows(parts, rims, p, ys))
            for n, y in enumerate(ys):
                part = product[:, n * 128 : n * 128 + 128]
                for q in range(2):
                    k = 192 * q
                    value = (
                        shifted(part[k : k + 64], -2)
                        + part[k + 64 : k + 128]
                        + shifted(part[k + 128 : k + 192], 2)
                    )
                    value = value * slope[p + 2 * q, y + 1]
                    if y < 0:
                        value = jnp.where(place[0] > 0, 0.0, value)
                    if y >= 8:
                        value = jnp.where(place[1] > 0, 0.0, value)
                    pre_grad[p + 2 * q, y + 1] = value.astype(BF)
    for c in range(3):
        turned = w1_full[c].astype(F32).T
        w1_turned[c] = jnp.concatenate([turned[64 * b : 64 * b + 64] for b in range(3)], 1)
    weights = w1_turned[:, pl.ds(mine, 16), :].reshape(48, 192).astype(BF)
    for z in range(4):
        for base in range(0, 8, 4):
            ys = range(base, base + 4)
            cells = jnp.concatenate(
                [jnp.concatenate([pre_grad[z, y + 2 - b] for b in range(3)], 0) for y in ys], 1
            )
            product = dot(weights, cells)
            for n, y in enumerate(ys):
                part = product[:, n * 128 : n * 128 + 128]
                value = shifted(part[:16], -1) + part[16:32] + shifted(part[32:48], 1)
                input_grad[z, y] = value.astype(BF)


def sum_kernel(shares, summed):
    summed[...] = jnp.broadcast_to(jnp.sum(shares[...], 0).astype(BF)[None], (64, 8, 128))


def spread_kernel(tiles, first, second):
    for g in range(4):
        for c in range(3):
            for half in range(2):
                t = g * 6 + c * 2 + half
                main = tiles[t].astype(F32)
                rest = tiles[24 + t % 12].astype(F32)
                parts = [main[:, :64], main[:, 64:], rest[:, :64] if t < 12 else rest[:, 64:]]
                for b in range(3):
                    if g < 3:
                        second[g, b, c, 8 * half : 8 * half + 8, :] = parts[b]
                    else:
                        first[b, c, 8 * half : 8 * half + 8, :] = parts[b]


SMEM = pl.BlockSpec(memory_space=pltpu.SMEM)
VMEM = pl.BlockSpec(memory_space=pltpu.VMEM)


def call(kernel, operands, outs, scratch=(), scalars=1, source=pltpu.VMEM, near=True, far=()):
    operands = list(operands)
    for n in range(scalars, len(operands)):
        space = pltpu.HBM if n in far else source
        operands[n] = pltpu.with_memory_space_constraint(operands[n], space)
    return pl.pallas_call(
        kernel,
        in_specs=[SMEM] * scalars + [VMEM] * (len(operands) - scalars),
        out_specs=tuple(VMEM for _ in outs),
        out_shape=tuple(
            pltpu.VMEM(shape, kind) if near else jax.ShapeDtypeStruct(shape, kind)
            for shape, kind in outs
        ),
        scratch_shapes=list(scratch),
        compiler_params=pltpu.CompilerParams(vmem_limit_bytes=16 << 20),
    )(*operands)


FORWARD = [(i, i + 1) for i in range(63)]
BACKWARD = [(i + 1, i) for i in range(63)]
ACROSS = [(i, 3 - i) for i in range(4)]


def per_device(volume, w_first, w_second, cotangent):
    block = lax.axis_index(BLOCKS)
    mine = lax.axis_index(FILT)
    place = jnp.stack([block == 0, block == 63, mine]).astype(jnp.int32)
    rows = ((32, 16, 128), BF)
    taps = ((18, 16, 128), BF)
    rim = ((60, 16, 128), BF)
    vol, down, up, part0, kernels0, own = call(
        prepare_kernel,
        (volume, cotangent, w_first, w_second),
        (((4, 8, 64, 128), BF), rim, rim, rows, taps, ((50, 16, 128), BF)),
        scalars=0,
        source=pltpu.HBM,
    )
    part2 = lax.ppermute(part0, "x_hi", SWAP)
    low = lax.ppermute(down, BLOCKS, FORWARD)
    high = lax.ppermute(up, BLOCKS, BACKWARD)
    kernels2 = lax.ppermute(kernels0, ("x_lo", "x_hi"), ACROSS)
    part1 = lax.ppermute(own, "core", SWAP)
    part3 = lax.ppermute(part2, "core", SWAP)
    kernels3 = lax.ppermute(kernels2, "core", SWAP)
    rim0 = jnp.concatenate([low[:12], high[:12]], 0)
    rim2 = lax.ppermute(rim0, "x_hi", SWAP)
    rim1 = lax.ppermute(rim0, "core", SWAP)
    rim3 = lax.ppermute(rim2, "core", SWAP)
    parts = (part0, part1, part2, part3)
    kernels = (kernels0, part1, kernels2, kernels3)
    rims = (rim0, rim1, rim2, rim3)
    hidden, slope, second, w2_turned = call(
        forward_kernel,
        (place, vol, low, high, part0) + kernels,
        (
            ((4, 12, 64, 128), BF),
            ((4, 10, 64, 128), F32),
            ((96, 384), F32),
            ((6, 64, 384), BF),
        ),
        [pltpu.VMEM((3, 64, 192), BF)],
    )
    (packed,) = call(
        first_grad_kernel,
        (place, vol, low, high) + parts + rims + (slope, second, w2_turned),
        (((64, 8, 128), F32),),
        [pltpu.VMEM((4, 8, 16, 128), BF)],
    )
    shares = lax.all_to_all(packed, BLOCKS, 0, 0)
    output, input_grad = call(
        outputs_kernel,
        (place, hidden) + parts + rims + (slope,) + kernels + (w2_turned,),
        (((4, 8, 16, 128), BF), ((4, 8, 16, 128), BF)),
        [
            pltpu.VMEM((4, 10, 64, 128), BF),
            pltpu.VMEM((3, 64, 192), BF),
            pltpu.VMEM((3, 64, 192), F32),
        ],
        far=(1, 6, 7, 8, 9, 11, 13, 14),
    )
    (summed,) = call(sum_kernel, (shares,), (((64, 8, 128), BF),), scalars=0)
    tiles = lax.all_to_all(summed, BLOCKS, 0, 0)
    first_grad, second_grad = call(
        spread_kernel,
        (tiles,),
        (((3, 3, 16, 64), F32), ((3, 3, 3, 16, 64), F32)),
        scalars=0,
        near=False,
    )
    return (output.transpose(2, 0, 1, 3), input_grad.transpose(2, 0, 1, 3), first_grad, second_grad)


def solution(mesh):
    fine = Mesh(mesh.devices.reshape(tuple(SPLIT.values())), tuple(SPLIT))
    return jax.shard_map(
        per_device,
        mesh=fine,
        in_specs=(
            P(None, None, BLOCKS, None),
            P(None, None, FILT, None),
            P(None, None, None, FILT, None),
            P(FILT, None, BLOCKS, None),
        ),
        out_specs=(
            P(FILT, None, BLOCKS, None),
            P(FILT, None, BLOCKS, None),
            P(None, None, FILT, None),
            P(None, None, None, FILT, None),
        ),
        check_vma=False,
    )
```

time: 94.2 us -> 76.1 us (0.81)
  the two profiles are of different devices: /device:TPU:4 before, /device:TPU:2 now
where the time goes in v2:
time: 76.1 us; the launch traced here: 75.7 us
  blocking collectives  24.2 us (32%)
  starting transfers between devices  23.1 us (30%)
  waiting for transfers between devices  13.3 us (17%)
  Pallas kernels  10.4 us (14%)
  local copies, waits for them, and re-layouts  3.85 us (5%)
  between operations  0.82 us (1%)
    all_to_all x1, blocking collectives, per_device(): shares = lax.all_to_all(packed, BLOCKS, 0, 0)  24.2 us
    pallas_call x6, Pallas kernels, call(): pl.pallas_call(kernel, in_specs=[SMEM] * scalars + [VMEM] * (len(operands...  10.4 us
    ppermute x1, starting transfers between devices, per_device(): high = lax.ppermute(up, BLOCKS, BACKWARD)  8.28 us
    all_to_all x1, waiting for transfers between devices, per_device(): tiles = lax.all_to_all(summed, BLOCKS, 0, 0)  5.77 us
    all_to_all x1, starting transfers between devices, per_device(): tiles = lax.all_to_all(summed, BLOCKS, 0, 0)  4.87 us
    ppermute x1, waiting for transfers between devices, per_device(): kernels2 = lax.ppermute(kernels0, ('x_lo', 'x_hi'), ACROSS)  4.76 us
    unnamed x22, local copies, waits for them, and re-layouts  3.84 us
    ppermute x1, starting transfers between devices, per_device(): low = lax.ppermute(down, BLOCKS, FORWARD)  3.83 us
  transfers between devices with their start and end apart: 11, of which 4 were waited for; matrix products, arithmetic and copies ran while one was open for 2% of the time, Pallas kernels for 7%

profile of v2, /device:TPU:2, one launch (start us, length us, event | category | flops | bytes accessed | tf_op | source)
XLA Modules:
  0.0 75.7 jit_solution(16463233006597582183)
XLA Ops:
  0.6 1.5 %shard_map.75 = (bf16[4,8,64,128]{3,2,1,0:T(8,128)(2,1)S(1)}, bf16[60,16,128]{2,1,0:T(8,128)(2,1)S(1)}, bf16[60,16,128]{2,1,0:T(8,128)(2,1)S(1)}, bf16[32,16,128...) custom-call(bf16[64,4,8,128]{3,2,1,0:T(8,128)(2,1)} %volume.1, ...), custom_call_target="tpu_custom_call" | custom-call | tf_op jit(solution)/shard_map/pallas_call | solution.py:364
  2.1 0.0 copy-start.5
  2.1 3.8 %collective-permute-start = (bf16[60,16,128]{2,1,0:T(8,128)(2,1)S(1)}, bf16[60,16,128]{2,1,0:T(8,128)(2,1)S(1)}, u32[]{:S(2)}, u32[]{:S(2)}) collective-permute-start(bf16[60,16,128]{2,1,0:T(8,128)(2,1)S(1)} %get-tuple-element.19), channel_id=1, source_target_pairs={{0,4},{4,8},{8,12},{12,16},{16,20},{20,24},{24,28},{28,32},{32,36}... | collective-permute-start | bytes 737288 | tf_op jit(solution)/shard_map/ppermute | solution.py:397
  6.0 8.3 %collective-permute-start.1 = (bf16[60,16,128]{2,1,0:T(8,128)(2,1)S(1)}, bf16[60,16,128]{2,1,0:T(8,128)(2,1)S(1)}, u32[]{:S(2)}, u32[]{:S(2)}) collective-permute-start(bf16[60,16,128]{2,1,0:T(8,128)(2,1)S(1)} %get-tuple-element.20), channel_id=1, source_target_pairs={{4,0},{8,4},{12,8},{16,12},{20,16},{24,20},{28,24},{32,28},{36,32}... | collective-permute-start | bytes 737288 | tf_op jit(solution)/shard_map/ppermute | solution.py:398
  14.3 2.5 %collective-permute-start.5 = (bf16[32,16,128]{2,1,0:T(8,128)(2,1)S(1)}, bf16[32,16,128]{2,1,0:T(8,128)(2,1)S(1)}, u32[]{:S(2)}, u32[]{:S(2)}) collective-permute-start(bf16[32,16,128]{2,1,0:T(8,128)(2,1)S(1)} %get-tuple-element.21.part0), channel_id=1, source_target_pairs={{0,2},{2,0},{1,3},{3,1},{4,6},{6,4},{5,7},{7,5},{8,10},{10,8},{9,1... | collective-permute-start | bytes 393224 | tf_op jit(solution)/shard_map/ppermute | solution.py:396
  16.8 1.5 %collective-permute-done.low = bf16[60,16,128]{2,1,0:T(8,128)(2,1)S(1)} collective-permute-done((bf16[60,16,128]{2,1,0:T(8,128)(2,1)S(1)}, bf16[60,16,128]{2,1,0:T(8,128)(2,1)S(1)}, u32[]{:S(2)}, u32[]{:S(2)}) %collective-permute-start) | collective-permute-done | bytes 245792 | tf_op jit(solution)/shard_map/ppermute | solution.py:397
  18.3 1.2 %collective-permute-done.1.high = bf16[60,16,128]{2,1,0:T(8,128)(2,1)S(1)} collective-permute-done((bf16[60,16,128]{2,1,0:T(8,128)(2,1)S(1)}, bf16[60,16,128]{2,1,0:T(8,128)(2,1)S(1)}, u32[]{:S(2)}, u32[]{:S(2)}) %collective-permute-start.1) | collective-permute-done | bytes 245792 | tf_op jit(solution)/shard_map/ppermute | solution.py:398
  19.5 0.0 copy-start
  19.5 2.5 %collective-permute-start.8 = (bf16[24,16,128]{2,1,0:T(8,128)(2,1)S(1)}, bf16[24,16,128]{2,1,0:T(8,128)(2,1)S(1)}, u32[]{:S(2)}, u32[]{:S(2)}) collective-permute-start(bf16[24,16,128]{2,1,0:T(8,128)(2,1)S(1)} %pad_maximum_fusion.rim0), channel_id=1, source_target_pairs={{0,2},{2,0},{1,3},{3,1},{4,6},{6,4},{5,7},{7,5},{8,10},{10,8},{9,1... | collective-permute-start | bytes 294920 | tf_op jit(solution)/shard_map/ppermute | solution.py:404
  22.0 0.0 collective-permute-start.3
  22.0 0.0 collective-permute-done.5.part2
  22.1 0.5 collective-permute-start.6
  22.6 4.8 %collective-permute-done.3.kernels2 = bf16[18,16,128]{2,1,0:T(8,128)(2,1)S(1)} collective-permute-done((bf16[18,16,128]{2,1,0:T(8,128)(2,1)S(1)}, bf16[18,16,128]{2,1,0:T(8,128)(2,1)S(1)}, u32[]{:S(2)}, u32[]{:S(2)}) %collective-permute-start.3) | collective-permute-done | bytes 73760 | tf_op jit(solution)/shard_map/ppermute | solution.py:399
  27.3 0.1 collective-permute-start.4
  27.4 0.6 copy-done.7
  28.0 0.4 collective-permute-start.7
  28.5 0.1 collective-permute-start.9
  28.6 0.1 pad_add_fusion.place
  28.7 0.0 copy-start.6
  28.7 0.9 %copy-done.6 = bf16[18,16,128]{2,1,0:T(8,128)(2,1)S(1)} copy-done((bf16[18,16,128]{2,1,0:T(8,128)(2,1)S(1)}, bf16[18,16,128]{2,1,0:T(8,128)(2,1)}, u32[]{:S(2)}) %copy-start.6) | copy-done | bytes 73752
  29.6 0.9 %copy-done.8 = bf16[18,16,128]{2,1,0:T(8,128)(2,1)S(1)} copy-done((bf16[18,16,128]{2,1,0:T(8,128)(2,1)S(1)}, bf16[18,16,128]{2,1,0:T(8,128)(2,1)}, u32[]{:S(2)}) %copy-start.8) | copy-done | bytes 73752
  30.5 2.1 %shard_map.76 = (bf16[4,12,64,128]{3,2,1,0:T(8,128)(2,1)S(1)}, f32[4,10,64,128]{3,2,1,0:T(8,128)S(1)}, f32[96,384]{1,0:T(8,128)S(1)}, bf16[6,64,384]{2,1,0:T(8,128)(2,1)S(1)}) custom-call(s32[3]{0:T(128)S(1)} %pad_add_fusion.place, bf16[4,8,64,128]{3,2,1,0:T(8,128)(2,1)S(1)} %get-tuple-element.18.vol, bf16[60,16,128]{2,1,0:T(8,128)(2,1)S(1)} %collective-permute-done.low, ...), custom_call_target="tpu_custom_call" | custom-call | tf_op jit(solution)/shard_map/pallas_call | solution.py:364
  32.6 0.0 copy-start.3
  32.6 1.9 %shard_map.78 = f32[64,8,128]{2,1,0:T(8,128)S(1)} custom-call(s32[3]{0:T(128)S(1)} %pad_add_fusion.place, bf16[4,8,64,128]{3,2,1,0:T(8,128)(2,1)S(1)} %get-tuple-element.18.vol, bf16[60,16,128]{2,1,0:T(8,128)(2,1)S(1)} %collective-permute-done.low, bf16[60,16,128]{2,1,0:T(8,128)(2,1)S(1)} %collective-permute-done.1.high, ...), custom_call_target="tpu_custom_call" | custom-call | tf_op jit(solution)/shard_map/pallas_call | solution.py:364
  34.5 24.2 %all_to_all.10.shares = f32[64,8,128]{2,1,0:T(8,128)S(1)} all-to-all(f32[64,8,128]{2,1,0:T(8,128)S(1)} %shard_map.78), channel_id=1, replica_groups=mesh['x_lo'=2,'y'=4,'z'=8,'x_hi'=2,'core'=2] {'x_lo','y','z'}, dimensions={0} | all-to-all | bytes 524288 | tf_op jit(solution)/shard_map/all_to_all | solution.py:427
  58.7 0.7 shard_map.79
  59.4 4.9 %all-to-all-start.1 = ((bf16[64,8,128]{2,1,0:T(8,128)(2,1)}), bf16[64,8,128]{2,1,0:T(8,128)(2,1)S(1)}, u32[]{:S(2)}, u32[]{:S(2)}) async-start(bf16[64,8,128]{2,1,0:T(8,128)(2,1)} %shard_map.79), calls=%async_computation.1 | async-start | bytes 262144 | tf_op jit(solution)/shard_map/all_to_all | solution.py:440
  64.3 3.4 %shard_map.77 = (bf16[4,8,16,128]{3,2,1,0:T(8,128)(2,1)S(1)}, bf16[4,8,16,128]{3,2,1,0:T(8,128)(2,1)S(1)}) custom-call(s32[3]{0:T(128)S(1)} %pad_add_fusion.place, bf16[4,12,64,128]{3,2,1,0:T(8,128)(2,1)} %copy-done.1, bf16[32,16,128]{2,1,0:T(8,128)(2,1)S(1)} %get-tuple-element.21.part0, bf16[50,16,128]{2,1,0:T(8,128)(2,1)S(1)} %collective-permute-done.2.kernels1.part1, ...), custom_call_target="tpu_custom_call" | custom-call | tf_op jit(solution)/shard_map/pallas_call | solution.py:364
  67.8 0.7 copy.8
  68.5 0.7 copy.9
  69.2 5.8 %all-to-all-done.1.tiles = bf16[64,8,128]{2,1,0:T(8,128)(2,1)S(1)} async-done(((bf16[64,8,128]{2,1,0:T(8,128)(2,1)}), bf16[64,8,128]{2,1,0:T(8,128)(2,1)S(1)}, u32[]{:S(2)}, u32[]{:S(2)}) %all-to-all-start.1) | async-done | bytes 131104 | tf_op jit(solution)/shard_map/all_to_all | solution.py:440
  74.9 0.8 %shard_map.80 = (f32[3,3,16,64]{3,2,1,0:T(8,128)}, f32[3,3,3,16,64]{4,3,2,1,0:T(8,128)}) custom-call(bf16[64,8,128]{2,1,0:T(8,128)(2,1)S(1)} %all-to-all-done.1.tiles), custom_call_target="tpu_custom_call" | custom-call | tf_op jit(solution)/shard_map/pallas_call | solution.py:364
  (23 shorter events, 0.1 us)
Async XLA Ops:
  2.1 26.5 %copy-start.5 = (bf16[18,16,128]{2,1,0:T(8,128)(2,1)}, bf16[18,16,128]{2,1,0:T(8,128)(2,1)S(1)}, u32[]{:S(2)}) copy-start(bf16[18,16,128]{2,1,0:T(8,128)(2,1)S(1)} %get-tuple-element.22.kernels0) | copy-start | bytes 221188
  2.1 16.1 %collective-permute-start = (bf16[60,16,128]{2,1,0:T(8,128)(2,1)S(1)}, bf16[60,16,128]{2,1,0:T(8,128)(2,1)S(1)}, u32[]{:S(2)}, u32[]{:S(2)}) collective-permute-start(bf16[60,16,128]{2,1,0:T(8,128)(2,1)S(1)} %get-tuple-element.19), channel_id=1, source_target_pairs={{0,4},{4,8},{8,12},{12,16},{16,20},{20,24},{24,28},{28,32},{32,36}... | collective-permute-start | bytes 737288 | tf_op jit(solution)/shard_map/ppermute | solution.py:397
  6.0 13.5 %collective-permute-start.1 = (bf16[60,16,128]{2,1,0:T(8,128)(2,1)S(1)}, bf16[60,16,128]{2,1,0:T(8,128)(2,1)S(1)}, u32[]{:S(2)}, u32[]{:S(2)}) collective-permute-start(bf16[60,16,128]{2,1,0:T(8,128)(2,1)S(1)} %get-tuple-element.20), channel_id=1, source_target_pairs={{4,0},{8,4},{12,8},{16,12},{20,16},{24,20},{28,24},{32,28},{36,32}... | collective-permute-start | bytes 737288 | tf_op jit(solution)/shard_map/ppermute | solution.py:398
  14.3 7.8 %collective-permute-start.5 = (bf16[32,16,128]{2,1,0:T(8,128)(2,1)S(1)}, bf16[32,16,128]{2,1,0:T(8,128)(2,1)S(1)}, u32[]{:S(2)}, u32[]{:S(2)}) collective-permute-start(bf16[32,16,128]{2,1,0:T(8,128)(2,1)S(1)} %get-tuple-element.21.part0), channel_id=1, source_target_pairs={{0,2},{2,0},{1,3},{3,1},{4,6},{6,4},{5,7},{7,5},{8,10},{10,8},{9,1... | collective-permute-start | bytes 393224 | tf_op jit(solution)/shard_map/ppermute | solution.py:396
  19.5 15.0 %copy-start = (bf16[24,16,128]{2,1,0:T(8,128)(2,1)}, bf16[24,16,128]{2,1,0:T(8,128)(2,1)S(1)}, u32[]{:S(2)}) copy-start(bf16[24,16,128]{2,1,0:T(8,128)(2,1)S(1)} %pad_maximum_fusion.rim0) | copy-start | bytes 294916
  19.5 8.9 %collective-permute-start.8 = (bf16[24,16,128]{2,1,0:T(8,128)(2,1)S(1)}, bf16[24,16,128]{2,1,0:T(8,128)(2,1)S(1)}, u32[]{:S(2)}, u32[]{:S(2)}) collective-permute-start(bf16[24,16,128]{2,1,0:T(8,128)(2,1)S(1)} %pad_maximum_fusion.rim0), channel_id=1, source_target_pairs={{0,2},{2,0},{1,3},{3,1},{4,6},{6,4},{5,7},{7,5},{8,10},{10,8},{9,1... | collective-permute-start | bytes 294920 | tf_op jit(solution)/shard_map/ppermute | solution.py:404
  22.0 6.6 %collective-permute-start.2 = (bf16[50,16,128]{2,1,0:T(8,128)(2,1)S(1)}, bf16[50,16,128]{2,1,0:T(8,128)(2,1)S(1)}, u32[]{:S(2)}, u32[]{:S(2)}) collective-permute-start(bf16[50,16,128]{2,1,0:T(8,128)(2,1)S(1)} %get-tuple-element.23), channel_id=1, source_target_pairs={{0,1},{1,0},{2,3},{3,2},{4,5},{5,4},{6,7},{7,6},{8,9},{9,8},{10,11... | collective-permute-start | bytes 614408 | tf_op jit(solution)/shard_map/ppermute | solution.py:400
  22.0 5.3 %collective-permute-start.3 = (bf16[18,16,128]{2,1,0:T(8,128)(2,1)S(1)}, bf16[18,16,128]{2,1,0:T(8,128)(2,1)S(1)}, u32[]{:S(2)}, u32[]{:S(2)}) collective-permute-start(bf16[18,16,128]{2,1,0:T(8,128)(2,1)S(1)} %get-tuple-element.22.kernels0), channel_id=1, source_target_pairs={{0,130},{2,128},{128,2},{130,0},{1,131},{3,129},{129,3},{131,1},{4... | collective-permute-start | bytes 221192 | tf_op jit(solution)/shard_map/ppermute | solution.py:399
  22.1 10.5 %collective-permute-start.6 = (bf16[32,16,128]{2,1,0:T(8,128)(2,1)S(1)}, bf16[32,16,128]{2,1,0:T(8,128)(2,1)S(1)}, u32[]{:S(2)}, u32[]{:S(2)}) collective-permute-start(bf16[32,16,128]{2,1,0:T(8,128)(2,1)S(1)} %collective-permute-done.5.part2), channel_id=1, source_target_pairs={{0,1},{1,0},{2,3},{3,2},{4,5},{5,4},{6,7},{7,6},{8,9},{9,8},{10,11... | collective-permute-start | bytes 393224 | tf_op jit(solution)/shard_map/ppermute | solution.py:401
  27.3 1.3 %collective-permute-start.4 = (bf16[18,16,128]{2,1,0:T(8,128)(2,1)S(1)}, bf16[18,16,128]{2,1,0:T(8,128)(2,1)S(1)}, u32[]{:S(2)}, u32[]{:S(2)}) collective-permute-start(bf16[18,16,128]{2,1,0:T(8,128)(2,1)S(1)} %collective-permute-done.3.kernels2), channel_id=1, source_target_pairs={{0,1},{1,0},{2,3},{3,2},{4,5},{5,4},{6,7},{7,6},{8,9},{9,8},{10,11... | collective-permute-start | bytes 221192 | tf_op jit(solution)/shard_map/ppermute | solution.py:402
  27.4 0.6 copy-start.7
  28.0 4.5 %collective-permute-start.7 = (bf16[24,16,128]{2,1,0:T(8,128)(2,1)S(1)}, bf16[24,16,128]{2,1,0:T(8,128)(2,1)S(1)}, u32[]{:S(2)}, u32[]{:S(2)}) collective-permute-start(bf16[24,16,128]{2,1,0:T(8,128)(2,1)S(1)} %pad_maximum_fusion.rim0), channel_id=1, source_target_pairs={{0,1},{1,0},{2,3},{3,2},{4,5},{5,4},{6,7},{7,6},{8,9},{9,8},{10,11... | collective-permute-start | bytes 294920 | tf_op jit(solution)/shard_map/ppermute | solution.py:405
  28.5 6.0 %copy-start.2 = (bf16[24,16,128]{2,1,0:T(8,128)(2,1)}, bf16[24,16,128]{2,1,0:T(8,128)(2,1)S(1)}, u32[]{:S(2)}) copy-start(bf16[24,16,128]{2,1,0:T(8,128)(2,1)S(1)} %collective-permute-done.8.rim2) | copy-start | bytes 294916
  28.5 4.1 %collective-permute-start.9 = (bf16[24,16,128]{2,1,0:T(8,128)(2,1)S(1)}, bf16[24,16,128]{2,1,0:T(8,128)(2,1)S(1)}, u32[]{:S(2)}, u32[]{:S(2)}) collective-permute-start(bf16[24,16,128]{2,1,0:T(8,128)(2,1)S(1)} %collective-permute-done.8.rim2), channel_id=1, source_target_pairs={{0,1},{1,0},{2,3},{3,2},{4,5},{5,4},{6,7},{7,6},{8,9},{9,8},{10,11... | collective-permute-start | bytes 294920 | tf_op jit(solution)/shard_map/ppermute | solution.py:406
  28.6 5.8 %copy-start.9 = (bf16[18,16,128]{2,1,0:T(8,128)(2,1)}, bf16[18,16,128]{2,1,0:T(8,128)(2,1)S(1)}, u32[]{:S(2)}) copy-start(bf16[18,16,128]{2,1,0:T(8,128)(2,1)S(1)} %collective-permute-done.4.kernels3) | copy-start | bytes 221188
  28.7 0.9 %copy-start.6 = (bf16[18,16,128]{2,1,0:T(8,128)(2,1)S(1)}, bf16[18,16,128]{2,1,0:T(8,128)(2,1)}, u32[]{:S(2)}) copy-start(bf16[18,16,128]{2,1,0:T(8,128)(2,1)} %copy-done.5) | copy-start | bytes 221188
  29.6 0.9 %copy-start.8 = (bf16[18,16,128]{2,1,0:T(8,128)(2,1)S(1)}, bf16[18,16,128]{2,1,0:T(8,128)(2,1)}, u32[]{:S(2)}) copy-start(bf16[18,16,128]{2,1,0:T(8,128)(2,1)} %copy-done.7) | copy-start | bytes 221188
  32.5 2.0 %copy-start.1 = (bf16[4,12,64,128]{3,2,1,0:T(8,128)(2,1)}, bf16[4,12,64,128]{3,2,1,0:T(8,128)(2,1)S(1)}, u32[]{:S(2)}) copy-start(bf16[4,12,64,128]{3,2,1,0:T(8,128)(2,1)S(1)} %get-tuple-element.24.hidden) | copy-start | bytes 2359300
  32.6 1.9 %copy-start.3 = (bf16[24,16,128]{2,1,0:T(8,128)(2,1)}, bf16[24,16,128]{2,1,0:T(8,128)(2,1)S(1)}, u32[]{:S(2)}) copy-start(bf16[24,16,128]{2,1,0:T(8,128)(2,1)S(1)} %collective-permute-done.7.rim1) | copy-start | bytes 294916
  32.6 1.9 %copy-start.4 = (bf16[24,16,128]{2,1,0:T(8,128)(2,1)}, bf16[24,16,128]{2,1,0:T(8,128)(2,1)S(1)}, u32[]{:S(2)}) copy-start(bf16[24,16,128]{2,1,0:T(8,128)(2,1)S(1)} %collective-permute-done.9.rim3) | copy-start | bytes 294916
  59.4 15.5 %all-to-all-start.1 = ((bf16[64,8,128]{2,1,0:T(8,128)(2,1)}), bf16[64,8,128]{2,1,0:T(8,128)(2,1)S(1)}, u32[]{:S(2)}, u32[]{:S(2)}) async-start(bf16[64,8,128]{2,1,0:T(8,128)(2,1)} %shard_map.79), calls=%async_computation.1 | async-start | bytes 262144 | tf_op jit(solution)/shard_map/all_to_all | solution.py:440

commit v3 on v2

v3 whole, which is shorter than its diff:
```python
import jax
import jax.numpy as jnp
from jax import lax
from jax.experimental import pallas as pl
from jax.experimental.pallas import tpu as pltpu
from jax.sharding import Mesh, PartitionSpec as P


BLOCKS = ("x_lo", "y", "z")
FILT = ("x_hi", "core")
SPLIT = {"x_lo": 2, "y": 4, "z": 8, "x_hi": 2, "core": 2}
BF = jnp.bfloat16
F32 = jnp.float32
SWAP = [(0, 1), (1, 0)]


def dot(left, right):
    return lax.dot_general(left, right, (((1,), (0,)), ((), ())), preferred_element_type=F32)


def dot_cells(left, right):
    return lax.dot_general(left, right, (((1,), (1,)), ((), ())), preferred_element_type=F32)


def shifted(value, amount):
    lane = lax.broadcasted_iota(jnp.int32, value.shape, 1)
    width = value.shape[1]
    moved = pltpu.roll(value, amount % width, 1)
    inside = lane >= amount if amount > 0 else lane < width + amount
    return jnp.where(inside, moved, 0.0)


def prepare_kernel(volume, cotangent, w_first, w_second, vol, near, far, grads, kernels, own):
    odd = lax.axis_index("z") & 1
    for z in range(4):
        rows = jnp.swapaxes(volume[:, z].astype(F32), 0, 1).astype(BF)
        vol[z] = rows
        mine = jnp.swapaxes(cotangent[:, z].astype(F32), 0, 1).astype(BF)
        grads[8 * z : 8 * z + 8] = mine
        own[8 * z : 8 * z + 8] = mine
        for n in range(3):
            k = 3 * z + n
            for edge, start in ((near, 5 * (1 - odd)), (far, 5 * odd)):
                edge[k] = grads[8 * z + start + n]
                edge[12 + 4 * k : 16 + 4 * k] = vol[z, start + n].reshape(4, 16, 128)
    strips = [w_first[b, c] for c in range(3) for b in range(3)]
    strips += [w_second[a, b, c] for a in range(3) for b in range(3) for c in range(3)]
    for n in range(18):
        pair = jnp.concatenate(strips[2 * n : 2 * n + 2], 1)
        kernels[n] = pair
        own[32 + n] = pair


def position():
    block = lax.axis_index(BLOCKS)
    return block == 0, block == 63, lax.axis_index(FILT)


def strip(kernels, base, n):
    k = base + 3 * (n // 2)
    if n % 2 == 0:
        return jnp.concatenate([kernels[k], kernels[k + 1][:, :64]], 1)
    return jnp.concatenate([kernels[k + 1][:, 64:], kernels[k + 2]], 1)


def volume_row(vol, halo, z, y):
    if 0 <= y < 8:
        return vol[z, y]
    return halo[z, y + 3 if y < 0 else y - 5]


def stacked_rows(vol, halo, z, y):
    return jnp.concatenate([volume_row(vol, halo, z, y + n) for n in (-1, 0, 1)], 0)


def build_halo(near, far, halo):
    odd = lax.axis_index("z") & 1
    for edge, start in ((near, 3 * (1 - odd)), (far, 3 * odd)):
        for z in range(4):
            for n in range(3):
                k = 12 + 4 * (3 * z + n)
                halo[z, start + n] = edge[k : k + 4].reshape(64, 128)


def build_first(spot, kernels, w1_full):
    for r in range(4):
        f = pl.multiple_of((spot ^ r) * 16, 16)
        for c in range(3):
            w1_full[c, pl.ds(f, 16), :] = strip(*kernels[r], c)


def forward_kernel(
    vol,
    near,
    far,
    part0,
    kernels0,
    kernels1,
    kernels2,
    kernels3,
    hidden_out,
    slope,
    grads,
    w1_full,
    w2_own,
    w2_turned,
    halo,
    hidden,
    leaving,
):
    first, last, spot = position()
    build_halo(near, far, halo)
    kernels = ((kernels0, 0), (kernels1, 32), (kernels2, 0), (kernels3, 0))
    build_first(spot, kernels, w1_full)
    w2_own[...] = jnp.concatenate(
        [
            jnp.concatenate(
                [
                    strip(kernels0, 0, 3 + 3 * (1 + q - z) + b)[:, 64 * c : 64 * c + 64]
                    for q in range(2)
                    for b in range(3)
                ],
                1,
            )
            for z in range(2)
            for c in range(3)
        ],
        0,
    )

    turned = jnp.concatenate(
        [
            jnp.concatenate([strip(*kernels[r], 3 + 3 * (1 + z - q) + b) for z in range(2)], 1)
            for b in range(3)
            for q in range(2)
            for r in range(4)
        ],
        0,
    )
    w2_turned[...] = turned.T.reshape(6, 64, 384)
    weights = w1_full[...].reshape(192, 192)
    copies = []
    for z in range(4):
        for base in range(-2, 10, 4):
            ys = range(base, base + 4)
            cells = jnp.concatenate([stacked_rows(vol, halo, z, y) for y in ys], 1)
            product = dot(weights, cells)
            for n, y in enumerate(ys):
                part = product[:, n * 128 : n * 128 + 128]
                pre = shifted(part[:64], 1) + part[64:128] + shifted(part[128:], -1)
                sigma = 1.0 / (1.0 + jnp.exp(-pre))
                value = pre * sigma
                steep = sigma * (1.0 + pre * (1.0 - sigma))
                if not 0 <= y < 8:
                    outside = first if y < 0 else last
                    value = jnp.where(outside, 0.0, value)
                    steep = jnp.where(outside, 0.0, steep)
                hidden[z, y + 2] = value.astype(BF)
                slope[z, y + 2] = steep
        copies.append(pltpu.make_async_copy(hidden.at[z], hidden_out.at[z], leaving.at[z]))
        copies[z].start()
    total = None
    for p in range(2):
        for base in range(0, 8, 4):
            ys = range(base, base + 4)
            left = []
            for y in ys:
                pieces = []
                for q in range(2):
                    own = part0[8 * (p + 2 * q) + y]
                    wide = own.astype(F32)
                    pieces += [shifted(wide, -2).astype(BF), own, shifted(wide, 2).astype(BF)]
                left.append(jnp.concatenate(pieces, 0))
            term = dot_cells(jnp.concatenate(left, 1), hidden_rows(hidden, p, ys))
            total = term if total is None else total + term
    grads[...] = total
    for copy in copies:
        copy.wait()


def hidden_rows(hidden, p, ys):
    return jnp.concatenate(
        [
            jnp.concatenate([hidden[p + 2 * q, y + 2 * b] for q in range(2) for b in range(3)], 0)
            for y in ys
        ],
        1,
    )


def grad_rows(parts, rims, p, ys, taps=range(3)):
    odd = lax.axis_index("z") & 1

    def grad_row(r, z, y):
        if 0 <= y < 8:
            return parts[r][8 * z + y]
        if rims is None:
            return jnp.zeros((16, 128), BF)
        return rims[r][12 * (1 - odd) + 3 * z + y + 3 if y < 0 else 12 * odd + 3 * z + y - 8]

    return jnp.concatenate(
        [
            jnp.concatenate(
                [
                    grad_row(r, p + 2 * q, y - 2 * (b - 1))
                    for b in taps
                    for q in range(2)
                    for r in range(4)
                ],
                0,
            )
            for y in ys
        ],
        1,
    )


def first_grad_kernel(
    vol, halo, part0, part1, part2, part3, slope, second, w2_turned, packed, own_grad, w2_mine
):
    parts = (part0, part1, part2, part3)
    mine = pl.multiple_of(position()[2] * 16, 16)
    w2_mine[...] = w2_turned[:, pl.ds(mine, 16), :].reshape(96, 384)
    for p in range(2):
        for ys in (range(-2, 0), range(4), range(4, 8), range(8, 10)):
            taps = range(3) if 0 <= ys[0] < 8 else range(0, 1) if ys[0] < 0 else range(2, 3)
            weights = w2_mine[:, 128 * taps[0] : 128 * (taps[-1] + 1)]
            product = dot(weights, grad_rows(parts, None, p, ys, taps))
            for n, y in enumerate(ys):
                part = product[:, n * 128 : n * 128 + 128]
                for q in range(2):
                    k = 48 * q
                    value = (
                        shifted(part[k : k + 16], -2)
                        + part[k + 16 : k + 32]
                        + shifted(part[k + 32 : k + 48], 2)
                    )
                    value = value * slope[p + 2 * q, y + 2, pl.ds(mine, 16), :]
                    own_grad[p + 2 * q, y + 2] = value.astype(BF)
    total = None
    for z in range(4):
        for base in range(-2, 10, 4):
            ys = range(base, base + 4)
            left = []
            for y in ys:
                own = own_grad[z, y + 2]
                wide = own.astype(F32)
                left.append(
                    jnp.concatenate([shifted(wide, -1).astype(BF), own, shifted(wide, 1).astype(BF)], 0)
                )
            source = jnp.concatenate([stacked_rows(vol, halo, z, y) for y in ys], 1)
            term = dot_cells(jnp.concatenate(left, 1), source)
            total = term if total is None else total + term
    raw = second[...]
    rows = jnp.concatenate(
        [raw[48:, :192], raw[:48, :192] + raw[48:, 192:], raw[:48, 192:], total], 0
    ) * (1.0 / 512.0)
    for k in range(24):
        packed[k] = rows[8 * k : 8 * k + 8, :128]
    for k in range(12):
        packed[24 + k] = jnp.concatenate(
            [rows[8 * k : 8 * k + 8, 128:], rows[96 + 8 * k : 104 + 8 * k, 128:]], 1
        )
    packed[36:] = jnp.zeros((28, 8, 128), F32)


def output_kernel(hidden, w2_own, out):
    weights = w2_own[...]
    for p in range(2):
        for base in range(0, 8, 4):
            ys = range(base, base + 4)
            product = dot(weights, hidden_rows(hidden, p, ys))
            for n, y in enumerate(ys):
                part = product[:, n * 128 : n * 128 + 128]
                for q in range(2):
                    k = 48 * q
                    value = (
                        shifted(part[k : k + 16], 2)
                        + part[k + 16 : k + 32]
                        + shifted(part[k + 32 : k + 48], -2)
                    )
                    out[p + 2 * q, y] = value.astype(BF)


def input_grad_kernel(
    part0,
    part1,
    part2,
    part3,
    rim0,
    rim1,
    rim2,
    rim3,
    slope,
    w1_full,
    w2_turned,
    input_grad,
    pre_grad,
    w1_turned,
):
    parts = (part0, part1, part2, part3)
    rims = (rim0, rim1, rim2, rim3)
    mine = pl.multiple_of(position()[2] * 16, 16)
    weights = w2_turned[...].reshape(384, 384)
    for p in range(2):
        for base in range(-1, 9, 2):
            ys = range(base, base + 2)
            product = dot(weights, grad_rows(parts, rims, p, ys))
            for n, y in enumerate(ys):
                part = product[:, n * 128 : n * 128 + 128]
                for q in range(2):
                    k = 192 * q
                    value = (
                        shifted(part[k : k + 64], -2)
                        + part[k + 64 : k + 128]
                        + shifted(part[k + 128 : k + 192], 2)
                    )
                    value = value * slope[p + 2 * q, y + 2]
                    pre_grad[p + 2 * q, y + 1] = value.astype(BF)
    for c in range(3):
        turned = w1_full[c].astype(F32).T
        w1_turned[c] = jnp.concatenate([turned[64 * b : 64 * b + 64] for b in range(3)], 1)
    weights = w1_turned[:, pl.ds(mine, 16), :].reshape(48, 192).astype(BF)
    for z in range(4):
        for base in range(0, 8, 4):
            ys = range(base, base + 4)
            cells = jnp.concatenate(
                [jnp.concatenate([pre_grad[z, y + 2 - b] for b in range(3)], 0) for y in ys], 1
            )
            product = dot(weights, cells)
            for n, y in enumerate(ys):
                part = product[:, n * 128 : n * 128 + 128]
                value = shifted(part[:16], -1) + part[16:32] + shifted(part[32:48], 1)
                input_grad[z, y] = value.astype(BF)


def sum_kernel(shares, summed):
    summed[...] = jnp.broadcast_to(jnp.sum(shares[...], 0).astype(BF)[None], (64, 8, 128))


def spread_kernel(tiles, first, second):
    for g in range(4):
        for c in range(3):
            for half in range(2):
                t = g * 6 + c * 2 + half
                main = tiles[t].astype(F32)
                rest = tiles[24 + t % 12].astype(F32)
                parts = [main[:, :64], main[:, 64:], rest[:, :64] if t < 12 else rest[:, 64:]]
                for b in range(3):
                    if g < 3:
                        second[g, b, c, 8 * half : 8 * half + 8, :] = parts[b]
                    else:
                        first[b, c, 8 * half : 8 * half + 8, :] = parts[b]


VMEM = pl.BlockSpec(memory_space=pltpu.VMEM)


def call(kernel, operands, outs, scratch=(), source=pltpu.VMEM, near=True, far=()):
    operands = list(operands)
    for n in range(len(operands)):
        space = pltpu.HBM if n in far else source
        operands[n] = pltpu.with_memory_space_constraint(operands[n], space)
    return pl.pallas_call(
        kernel,
        in_specs=[VMEM] * len(operands),
        out_specs=tuple(
            pl.BlockSpec(memory_space=out[2] if len(out) > 2 else pltpu.VMEM) for out in outs
        ),
        out_shape=tuple(
            (out[2] if len(out) > 2 else pltpu.VMEM)(*out[:2])
            if near
            else jax.ShapeDtypeStruct(*out[:2])
            for out in outs
        ),
        scratch_shapes=list(scratch),
        compiler_params=pltpu.CompilerParams(vmem_limit_bytes=16 << 20),
    )(*operands)


PAIRS = [(i, i ^ 1) for i in range(64)]
GAPS = [pair for i in range(1, 63, 2) for pair in ((i, i + 1), (i + 1, i))]
ACROSS = [(i, 3 - i) for i in range(4)]


def per_device(volume, w_first, w_second, cotangent):
    rows = ((32, 16, 128), BF)
    taps = ((18, 16, 128), BF)
    edge = ((60, 16, 128), BF)
    vol, near, far, part0, kernels0, own = call(
        prepare_kernel,
        (volume, cotangent, w_first, w_second),
        (((4, 8, 64, 128), BF), edge, edge, rows, taps, ((50, 16, 128), BF)),
        source=pltpu.HBM,
    )
    kernels2 = lax.ppermute(kernels0, ("x_lo", "x_hi"), ACROSS)
    part2 = lax.ppermute(part0, "x_hi", SWAP)
    near = lax.ppermute(near, BLOCKS, PAIRS)
    far = lax.ppermute(far, BLOCKS, GAPS)
    part1 = lax.ppermute(own, "core", SWAP)
    part3 = lax.ppermute(part2, "core", SWAP)
    kernels3 = lax.ppermute(kernels2, "core", SWAP)
    rim0 = jnp.concatenate([near[:12], far[:12]], 0)
    rim1 = lax.ppermute(rim0, "core", SWAP)
    rim2 = lax.ppermute(rim0, "x_hi", SWAP)
    rim3 = lax.ppermute(rim2, "core", SWAP)
    parts = (part0, part1, part2, part3)
    rims = (rim0, rim1, rim2, rim3)
    hidden, slope, second, w1_full, w2_own, w2_turned, halo = call(
        forward_kernel,
        (vol, near, far, part0, kernels0, part1, kernels2, kernels3),
        (
            ((4, 12, 64, 128), BF, pltpu.HBM),
            ((4, 12, 64, 128), F32),
            ((96, 384), F32),
            ((3, 64, 192), BF),
            ((96, 384), BF),
            ((6, 64, 384), BF),
            ((4, 6, 64, 128), BF),
        ),
        [pltpu.VMEM((4, 12, 64, 128), BF), pltpu.SemaphoreType.DMA((4,))],
    )
    (packed,) = call(
        first_grad_kernel,
        (vol, halo) + parts + (slope, second, w2_turned),
        (((64, 8, 128), F32),),
        [pltpu.VMEM((4, 12, 16, 128), BF), pltpu.VMEM((96, 384), BF)],
    )
    shares = lax.all_to_all(packed, BLOCKS, 0, 0)
    (output,) = call(output_kernel, (hidden, w2_own), (((4, 8, 16, 128), BF),), far=(0,))
    (input_grad,) = call(
        input_grad_kernel,
        parts + rims + (slope, w1_full, w2_turned),
        (((4, 8, 16, 128), BF),),
        [pltpu.VMEM((4, 10, 64, 128), BF), pltpu.VMEM((3, 64, 192), F32)],
    )
    (summed,) = call(sum_kernel, (shares,), (((64, 8, 128), BF),))
    tiles = lax.all_to_all(summed, BLOCKS, 0, 0)
    first_grad, second_grad = call(
        spread_kernel, (tiles,), (((3, 3, 16, 64), F32), ((3, 3, 3, 16, 64), F32)), near=False
    )
    return (output.transpose(2, 0, 1, 3), input_grad.transpose(2, 0, 1, 3), first_grad, second_grad)


def solution(mesh):
    fine = Mesh(mesh.devices.reshape(tuple(SPLIT.values())), tuple(SPLIT))
    return jax.shard_map(
        per_device,
        mesh=fine,
        in_specs=(
            P(None, None, BLOCKS, None),
            P(None, None, FILT, None),
            P(None, None, None, FILT, None),
            P(FILT, None, BLOCKS, None),
        ),
        out_specs=(
            P(FILT, None, BLOCKS, None),
            P(FILT, None, BLOCKS, None),
            P(None, None, FILT, None),
            P(None, None, None, FILT, None),
        ),
        check_vma=False,
    )
```

time: 76.1 us -> 66.7 us (0.88)
  the two profiles are of different devices: /device:TPU:2 before, /device:TPU:1 now
where the time goes in v3:
time: 66.7 us; the launch traced here: 66.4 us
  starting transfers between devices  38.7 us (58%)
  waiting for transfers between devices  14.1 us (21%)
  Pallas kernels  11.5 us (17%)
  local copies, waits for them, and re-layouts  1.39 us (2%)
  between operations  0.73 us (1%)
    pallas_call x7, Pallas kernels, call(): pl.pallas_call(kernel, in_specs=[VMEM] * len(operands), out_specs=tuple((...  11.5 us
    all_to_all x1, waiting for transfers between devices, per_device(): shares = lax.all_to_all(packed, BLOCKS, 0, 0)  11 us
    ppermute x1, starting transfers between devices, per_device(): kernels2 = lax.ppermute(kernels0, ('x_lo', 'x_hi'), ACROSS)  8.86 us
    all_to_all x1, starting transfers between devices, per_device(): shares = lax.all_to_all(packed, BLOCKS, 0, 0)  6.79 us
    ppermute x1, starting transfers between devices, per_device(): rim3 = lax.ppermute(rim2, 'core', SWAP)  4.67 us
    all_to_all x1, starting transfers between devices, per_device(): tiles = lax.all_to_all(summed, BLOCKS, 0, 0)  4.62 us
    ppermute x1, starting transfers between devices, per_device(): part2 = lax.ppermute(part0, 'x_hi', SWAP)  3.65 us
    ppermute x1, starting transfers between devices, per_device(): rim2 = lax.ppermute(rim0, 'x_hi', SWAP)  3.19 us
  transfers between devices with their start and end apart: 12, of which 3 were waited for; matrix products, arithmetic and copies ran while one was open for 2% of the time, Pallas kernels for 9%

profile of v3, /device:TPU:1, one launch (start us, length us, event | category | flops | bytes accessed | tf_op | source)
XLA Modules:
  0.0 66.4 jit_solution(10395618791000945065)
XLA Ops:
  0.6 1.5 %shard_map.75 = (bf16[4,8,64,128]{3,2,1,0:T(8,128)(2,1)S(1)}, bf16[60,16,128]{2,1,0:T(8,128)(2,1)S(1)}, bf16[60,16,128]{2,1,0:T(8,128)(2,1)S(1)}, bf16[32,16,128...) custom-call(bf16[64,4,8,128]{3,2,1,0:T(8,128)(2,1)} %volume.1, ...), custom_call_target="tpu_custom_call" | custom-call | tf_op jit(solution)/shard_map/pallas_call | solution.py:364
  2.2 3.6 %collective-permute-start.5 = (bf16[32,16,128]{2,1,0:T(8,128)(2,1)S(1)}, bf16[32,16,128]{2,1,0:T(8,128)(2,1)S(1)}, u32[]{:S(2)}, u32[]{:S(2)}) collective-permute-start(bf16[32,16,128]{2,1,0:T(8,128)(2,1)S(1)} %get-tuple-element.22.part0), channel_id=1, source_target_pairs={{0,2},{2,0},{1,3},{3,1},{4,6},{6,4},{5,7},{7,5},{8,10},{10,8},{9,1... | collective-permute-start | bytes 393224 | tf_op jit(solution)/shard_map/ppermute | solution.py:397
  5.8 1.6 %collective-permute-start = (bf16[60,16,128]{2,1,0:T(8,128)(2,1)S(1)}, bf16[60,16,128]{2,1,0:T(8,128)(2,1)S(1)}, u32[]{:S(2)}, u32[]{:S(2)}) collective-permute-start(bf16[60,16,128]{2,1,0:T(8,128)(2,1)S(1)} %get-tuple-element.20), channel_id=1, source_target_pairs={{0,4},{4,0},{8,12},{12,8},{16,20},{20,16},{24,28},{28,24},{32,36},... | collective-permute-start | bytes 737288 | tf_op jit(solution)/shard_map/ppermute | solution.py:398
  7.4 0.7 %collective-permute-start.1 = (bf16[60,16,128]{2,1,0:T(8,128)(2,1)S(1)}, bf16[60,16,128]{2,1,0:T(8,128)(2,1)S(1)}, u32[]{:S(2)}, u32[]{:S(2)}) collective-permute-start(bf16[60,16,128]{2,1,0:T(8,128)(2,1)S(1)} %get-tuple-element.21), channel_id=1, source_target_pairs={{4,8},{8,4},{12,16},{16,12},{20,24},{24,20},{28,32},{32,28},{36,40... | collective-permute-start | bytes 737288 | tf_op jit(solution)/shard_map/ppermute | solution.py:399
  8.1 1.3 %collective-permute-start.2 = (bf16[50,16,128]{2,1,0:T(8,128)(2,1)S(1)}, bf16[50,16,128]{2,1,0:T(8,128)(2,1)S(1)}, u32[]{:S(2)}, u32[]{:S(2)}) collective-permute-start(bf16[50,16,128]{2,1,0:T(8,128)(2,1)S(1)} %get-tuple-element.24), channel_id=1, source_target_pairs={{0,1},{1,0},{2,3},{3,2},{4,5},{5,4},{6,7},{7,6},{8,9},{9,8},{10,11... | collective-permute-start | bytes 614408 | tf_op jit(solution)/shard_map/ppermute | solution.py:400
  9.4 8.9 %collective-permute-start.3 = (bf16[18,16,128]{2,1,0:T(8,128)(2,1)S(1)}, bf16[18,16,128]{2,1,0:T(8,128)(2,1)S(1)}, u32[]{:S(2)}, u32[]{:S(2)}) collective-permute-start(bf16[18,16,128]{2,1,0:T(8,128)(2,1)S(1)} %get-tuple-element.23.kernels0), channel_id=1, source_target_pairs={{0,130},{2,128},{128,2},{130,0},{1,131},{3,129},{129,3},{131,1},{4... | collective-permute-start | bytes 221192 | tf_op jit(solution)/shard_map/ppermute | solution.py:396
  18.3 0.0 collective-permute-done.5.part2
  18.3 0.4 collective-permute-start.6
  18.7 2.2 %collective-permute-done.3.kernels2 = bf16[18,16,128]{2,1,0:T(8,128)(2,1)S(1)} collective-permute-done((bf16[18,16,128]{2,1,0:T(8,128)(2,1)S(1)}, bf16[18,16,128]{2,1,0:T(8,128)(2,1)S(1)}, u32[]{:S(2)}, u32[]{:S(2)}) %collective-permute-start.3) | collective-permute-done | bytes 73760 | tf_op jit(solution)/shard_map/ppermute | solution.py:396
  20.8 0.7 %collective-permute-start.4 = (bf16[18,16,128]{2,1,0:T(8,128)(2,1)S(1)}, bf16[18,16,128]{2,1,0:T(8,128)(2,1)S(1)}, u32[]{:S(2)}, u32[]{:S(2)}) collective-permute-start(bf16[18,16,128]{2,1,0:T(8,128)(2,1)S(1)} %collective-permute-done.3.kernels2), channel_id=1, source_target_pairs={{0,1},{1,0},{2,3},{3,2},{4,5},{5,4},{6,7},{7,6},{8,9},{9,8},{10,11... | collective-permute-start | bytes 221192 | tf_op jit(solution)/shard_map/ppermute | solution.py:402
  21.5 0.9 %collective-permute-done.4.kernels3 = bf16[18,16,128]{2,1,0:T(8,128)(2,1)S(1)} collective-permute-done((bf16[18,16,128]{2,1,0:T(8,128)(2,1)S(1)}, bf16[18,16,128]{2,1,0:T(8,128)(2,1)S(1)}, u32[]{:S(2)}, u32[]{:S(2)}) %collective-permute-start.4) | collective-permute-done | bytes 73760 | tf_op jit(solution)/shard_map/ppermute | solution.py:402
  22.4 0.0 collective-permute-done.2.kernels1.part1
  22.4 0.0 collective-permute-done.near
  22.4 0.0 collective-permute-done.1.far
  22.4 2.4 %shard_map.76 = (bf16[4,12,64,128]{3,2,1,0:T(8,128)(2,1)}, f32[4,12,64,128]{3,2,1,0:T(8,128)S(1)}, f32[96,384]{1,0:T(8,128)S(1)}, bf16[3,64,192]{2,1,0:T(8,128)(...) custom-call(bf16[4,8,64,128]{3,2,1,0:T(8,128)(2,1)S(1)} %get-tuple-eleme, ...), custom_call_target="tpu_custom_call" | custom-call | tf_op jit(solution)/shard_map/pallas_call | solution.py:364
  24.9 0.0 collective-permute-done.6.part3
  24.9 2.7 %shard_map.79 = f32[64,8,128]{2,1,0:T(8,128)} custom-call(bf16[4,8,64,128]{3,2,1,0:T(8,128)(2,1)S(1)} %get-tuple-element.19.vol, bf16[4,6,64,128]{3,2,1,0:T(8,128)(2,1)S(1)} %get-tuple-element.30.halo, bf16[32,16,128]{2,1,0:T(8,128)(2,1)S(1)} %get-tuple-element.22.part0, bf16[50,16,128]{2,1,0:T(8,128)(2,1)S(1)} %collective-permute-done.2.kernels1.part1, ...), custom_call_target="tpu_custom_call" | custom-call | tf_op jit(solution)/shard_map/pallas_call | solution.py:364
  27.6 6.8 %all-to-all-start = ((f32[64,8,128]{2,1,0:T(8,128)}), f32[64,8,128]{2,1,0:T(8,128)S(1)}, u32[]{:S(2)}, u32[]{:S(2)}) async-start(f32[64,8,128]{2,1,0:T(8,128)} %shard_map.79), calls=%async_computation | async-start | bytes 524288 | tf_op jit(solution)/shard_map/all_to_all | solution.py:429
  34.4 11.0 %all-to-all-done.shares = f32[64,8,128]{2,1,0:T(8,128)S(1)} async-done(((f32[64,8,128]{2,1,0:T(8,128)}), f32[64,8,128]{2,1,0:T(8,128)S(1)}, u32[]{:S(2)}, u32[]{:S(2)}) %all-to-all-start) | async-done | bytes 262176 | tf_op jit(solution)/shard_map/all_to_all | solution.py:429
  45.4 0.7 %shard_map.80 = bf16[64,8,128]{2,1,0:T(8,128)(2,1)} custom-call(f32[64,8,128]{2,1,0:T(8,128)S(1)} %all-to-all-done.shares), custom_call_target="tpu_custom_call" | custom-call | tf_op jit(solution)/shard_map/pallas_call | solution.py:364
  46.1 4.6 %all-to-all-start.1 = ((bf16[64,8,128]{2,1,0:T(8,128)(2,1)}), bf16[64,8,128]{2,1,0:T(8,128)(2,1)S(1)}, u32[]{:S(2)}, u32[]{:S(2)}) async-start(bf16[64,8,128]{2,1,0:T(8,128)(2,1)} %shard_map.80), calls=%async_computation.1 | async-start | bytes 262144 | tf_op jit(solution)/shard_map/all_to_all | solution.py:438
  50.8 3.2 %collective-permute-start.8 = (bf16[24,16,128]{2,1,0:T(8,128)(2,1)S(1)}, bf16[24,16,128]{2,1,0:T(8,128)(2,1)S(1)}, u32[]{:S(2)}, u32[]{:S(2)}) collective-permute-start(bf16[24,16,128]{2,1,0:T(8,128)(2,1)S(1)} %pad_maximum_fusion.rim0), channel_id=1, source_target_pairs={{0,2},{2,0},{1,3},{3,1},{4,6},{6,4},{5,7},{7,5},{8,10},{10,8},{9,1... | collective-permute-start | bytes 294920 | tf_op jit(solution)/shard_map/ppermute | solution.py:405
  54.0 2.3 %collective-permute-start.7 = (bf16[24,16,128]{2,1,0:T(8,128)(2,1)S(1)}, bf16[24,16,128]{2,1,0:T(8,128)(2,1)S(1)}, u32[]{:S(2)}, u32[]{:S(2)}) collective-permute-start(bf16[24,16,128]{2,1,0:T(8,128)(2,1)S(1)} %pad_maximum_fusion.rim0), channel_id=1, source_target_pairs={{0,1},{1,0},{2,3},{3,2},{4,5},{5,4},{6,7},{7,6},{8,9},{9,8},{10,11... | collective-permute-start | bytes 294920 | tf_op jit(solution)/shard_map/ppermute | solution.py:404
  56.2 0.0 collective-permute-done.8.rim2
  56.2 4.7 %collective-permute-start.9 = (bf16[24,16,128]{2,1,0:T(8,128)(2,1)S(1)}, bf16[24,16,128]{2,1,0:T(8,128)(2,1)S(1)}, u32[]{:S(2)}, u32[]{:S(2)}) collective-permute-start(bf16[24,16,128]{2,1,0:T(8,128)(2,1)S(1)} %collective-permute-done.8.rim2), channel_id=1, source_target_pairs={{0,1},{1,0},{2,3},{3,2},{4,5},{5,4},{6,7},{7,6},{8,9},{9,8},{10,11... | collective-permute-start | bytes 294920 | tf_op jit(solution)/shard_map/ppermute | solution.py:406
  60.9 1.6 %shard_map.77 = bf16[4,8,16,128]{3,2,1,0:T(8,128)(2,1)S(1)} custom-call(bf16[4,12,64,128]{3,2,1,0:T(8,128)(2,1)} %get-tuple-element.25.hidden, bf16[96,384]{1,0:T(8,128)(2,1)S(1)} %get-tuple-element.26.w2_own), custom_call_target="tpu_custom_call" | custom-call | tf_op jit(solution)/shard_map/pallas_call | solution.py:364
  62.6 0.7 %copy.8 = bf16[16,4,8,128]{3,2,1,0:T(8,128)(2,1)} copy(bf16[16,4,8,128]{3,0,2,1:T(8,128)(2,1)S(1)} %bitcast.3) | data formatting | bytes 262144
  63.2 0.0 collective-permute-done.7.rim1
  63.2 0.0 collective-permute-done.9.rim3
  63.2 1.7 %shard_map.78 = bf16[4,8,16,128]{3,2,1,0:T(8,128)(2,1)S(1)} custom-call(bf16[32,16,128]{2,1,0:T(8,128)(2,1)S(1)} %get-tuple-element.22.part0, bf16[50,16,128]{2,1,0:T(8,128)(2,1)S(1)} %collective-permute-done.2.kernels1.part1, bf16[32,16,128]{2,1,0:T(8,128)(2,1)S(1)} %collective-permute-done.5.part2, bf16[32,16,128]{2,1,0:T(8,128)(2,1)S(1)} %collective-permute-done.6.part3, ...), custom_call_target="tpu_custom_call" | custom-call | tf_op jit(solution)/shard_map/pallas_call | solution.py:364
  64.9 0.7 %copy.9 = bf16[16,4,8,128]{3,2,1,0:T(8,128)(2,1)} copy(bf16[16,4,8,128]{3,0,2,1:T(8,128)(2,1)S(1)} %bitcast.2) | data formatting | bytes 262144
  65.6 0.8 %shard_map.81 = (f32[3,3,16,64]{3,2,1,0:T(8,128)}, f32[3,3,3,16,64]{4,3,2,1,0:T(8,128)}) custom-call(bf16[64,8,128]{2,1,0:T(8,128)(2,1)S(1)} %all-to-all-done.1.tiles), custom_call_target="tpu_custom_call" | custom-call | tf_op jit(solution)/shard_map/pallas_call | solution.py:364
  (4 shorter events, 0.0 us)
Async XLA Ops:
  2.2 16.1 %collective-permute-start.5 = (bf16[32,16,128]{2,1,0:T(8,128)(2,1)S(1)}, bf16[32,16,128]{2,1,0:T(8,128)(2,1)S(1)}, u32[]{:S(2)}, u32[]{:S(2)}) collective-permute-start(bf16[32,16,128]{2,1,0:T(8,128)(2,1)S(1)} %get-tuple-element.22.part0), channel_id=1, source_target_pairs={{0,2},{2,0},{1,3},{3,1},{4,6},{6,4},{5,7},{7,5},{8,10},{10,8},{9,1... | collective-permute-start | bytes 393224 | tf_op jit(solution)/shard_map/ppermute | solution.py:397
  5.8 16.6 %collective-permute-start = (bf16[60,16,128]{2,1,0:T(8,128)(2,1)S(1)}, bf16[60,16,128]{2,1,0:T(8,128)(2,1)S(1)}, u32[]{:S(2)}, u32[]{:S(2)}) collective-permute-start(bf16[60,16,128]{2,1,0:T(8,128)(2,1)S(1)} %get-tuple-element.20), channel_id=1, source_target_pairs={{0,4},{4,0},{8,12},{12,8},{16,20},{20,16},{24,28},{28,24},{32,36},... | collective-permute-start | bytes 737288 | tf_op jit(solution)/shard_map/ppermute | solution.py:398
  7.4 15.0 %collective-permute-start.1 = (bf16[60,16,128]{2,1,0:T(8,128)(2,1)S(1)}, bf16[60,16,128]{2,1,0:T(8,128)(2,1)S(1)}, u32[]{:S(2)}, u32[]{:S(2)}) collective-permute-start(bf16[60,16,128]{2,1,0:T(8,128)(2,1)S(1)} %get-tuple-element.21), channel_id=1, source_target_pairs={{4,8},{8,4},{12,16},{16,12},{20,24},{24,20},{28,32},{32,28},{36,40... | collective-permute-start | bytes 737288 | tf_op jit(solution)/shard_map/ppermute | solution.py:399
  8.1 14.3 %collective-permute-start.2 = (bf16[50,16,128]{2,1,0:T(8,128)(2,1)S(1)}, bf16[50,16,128]{2,1,0:T(8,128)(2,1)S(1)}, u32[]{:S(2)}, u32[]{:S(2)}) collective-permute-start(bf16[50,16,128]{2,1,0:T(8,128)(2,1)S(1)} %get-tuple-element.24), channel_id=1, source_target_pairs={{0,1},{1,0},{2,3},{3,2},{4,5},{5,4},{6,7},{7,6},{8,9},{9,8},{10,11... | collective-permute-start | bytes 614408 | tf_op jit(solution)/shard_map/ppermute | solution.py:400
  9.4 11.4 %collective-permute-start.3 = (bf16[18,16,128]{2,1,0:T(8,128)(2,1)S(1)}, bf16[18,16,128]{2,1,0:T(8,128)(2,1)S(1)}, u32[]{:S(2)}, u32[]{:S(2)}) collective-permute-start(bf16[18,16,128]{2,1,0:T(8,128)(2,1)S(1)} %get-tuple-element.23.kernels0), channel_id=1, source_target_pairs={{0,130},{2,128},{128,2},{130,0},{1,131},{3,129},{129,3},{131,1},{4... | collective-permute-start | bytes 221192 | tf_op jit(solution)/shard_map/ppermute | solution.py:396
  18.3 6.6 %collective-permute-start.6 = (bf16[32,16,128]{2,1,0:T(8,128)(2,1)S(1)}, bf16[32,16,128]{2,1,0:T(8,128)(2,1)S(1)}, u32[]{:S(2)}, u32[]{:S(2)}) collective-permute-start(bf16[32,16,128]{2,1,0:T(8,128)(2,1)S(1)} %collective-permute-done.5.part2), channel_id=1, source_target_pairs={{0,1},{1,0},{2,3},{3,2},{4,5},{5,4},{6,7},{7,6},{8,9},{9,8},{10,11... | collective-permute-start | bytes 393224 | tf_op jit(solution)/shard_map/ppermute | solution.py:401
  20.8 1.6 %collective-permute-start.4 = (bf16[18,16,128]{2,1,0:T(8,128)(2,1)S(1)}, bf16[18,16,128]{2,1,0:T(8,128)(2,1)S(1)}, u32[]{:S(2)}, u32[]{:S(2)}) collective-permute-start(bf16[18,16,128]{2,1,0:T(8,128)(2,1)S(1)} %collective-permute-done.3.kernels2), channel_id=1, source_target_pairs={{0,1},{1,0},{2,3},{3,2},{4,5},{5,4},{6,7},{7,6},{8,9},{9,8},{10,11... | collective-permute-start | bytes 221192 | tf_op jit(solution)/shard_map/ppermute | solution.py:402
  27.6 17.8 %all-to-all-start = ((f32[64,8,128]{2,1,0:T(8,128)}), f32[64,8,128]{2,1,0:T(8,128)S(1)}, u32[]{:S(2)}, u32[]{:S(2)}) async-start(f32[64,8,128]{2,1,0:T(8,128)} %shard_map.79), calls=%async_computation | async-start | bytes 524288 | tf_op jit(solution)/shard_map/all_to_all | solution.py:429
  46.1 19.5 %all-to-all-start.1 = ((bf16[64,8,128]{2,1,0:T(8,128)(2,1)}), bf16[64,8,128]{2,1,0:T(8,128)(2,1)S(1)}, u32[]{:S(2)}, u32[]{:S(2)}) async-start(bf16[64,8,128]{2,1,0:T(8,128)(2,1)} %shard_map.80), calls=%async_computation.1 | async-start | bytes 262144 | tf_op jit(solution)/shard_map/all_to_all | solution.py:438
  50.8 5.4 %collective-permute-start.8 = (bf16[24,16,128]{2,1,0:T(8,128)(2,1)S(1)}, bf16[24,16,128]{2,1,0:T(8,128)(2,1)S(1)}, u32[]{:S(2)}, u32[]{:S(2)}) collective-permute-start(bf16[24,16,128]{2,1,0:T(8,128)(2,1)S(1)} %pad_maximum_fusion.rim0), channel_id=1, source_target_pairs={{0,2},{2,0},{1,3},{3,1},{4,6},{6,4},{5,7},{7,5},{8,10},{10,8},{9,1... | collective-permute-start | bytes 294920 | tf_op jit(solution)/shard_map/ppermute | solution.py:405
  54.0 9.3 %collective-permute-start.7 = (bf16[24,16,128]{2,1,0:T(8,128)(2,1)S(1)}, bf16[24,16,128]{2,1,0:T(8,128)(2,1)S(1)}, u32[]{:S(2)}, u32[]{:S(2)}) collective-permute-start(bf16[24,16,128]{2,1,0:T(8,128)(2,1)S(1)} %pad_maximum_fusion.rim0), channel_id=1, source_target_pairs={{0,1},{1,0},{2,3},{3,2},{4,5},{5,4},{6,7},{7,6},{8,9},{9,8},{10,11... | collective-permute-start | bytes 294920 | tf_op jit(solution)/shard_map/ppermute | solution.py:404
  56.2 7.0 %collective-permute-start.9 = (bf16[24,16,128]{2,1,0:T(8,128)(2,1)S(1)}, bf16[24,16,128]{2,1,0:T(8,128)(2,1)S(1)}, u32[]{:S(2)}, u32[]{:S(2)}) collective-permute-start(bf16[24,16,128]{2,1,0:T(8,128)(2,1)S(1)} %collective-permute-done.8.rim2), channel_id=1, source_target_pairs={{0,1},{1,0},{2,3},{3,2},{4,5},{5,4},{6,7},{7,6},{8,9},{9,8},{10,11... | collective-permute-start | bytes 294920 | tf_op jit(solution)/shard_map/ppermute | solution.py:406

commit v4 on v3

--- a/solution.py
+++ b/solution.py
@@ -255,13 +255,14 @@
     rows = jnp.concatenate(
         [raw[48:, :192], raw[:48, :192] + raw[48:, 192:], raw[:48, 192:], total], 0
     ) * (1.0 / 512.0)
+    rows = rows.astype(BF)
     for k in range(24):
         packed[k] = rows[8 * k : 8 * k + 8, :128]
     for k in range(12):
         packed[24 + k] = jnp.concatenate(
             [rows[8 * k : 8 * k + 8, 128:], rows[96 + 8 * k : 104 + 8 * k, 128:]], 1
         )
-    packed[36:] = jnp.zeros((28, 8, 128), F32)
+    packed[36:] = jnp.zeros((28, 8, 128), BF)
 
 
 def output_kernel(hidden, w2_own, out):
@@ -335,7 +336,7 @@
 
 
 def sum_kernel(shares, summed):
-    summed[...] = jnp.broadcast_to(jnp.sum(shares[...], 0).astype(BF)[None], (64, 8, 128))
+    summed[...] = jnp.broadcast_to(jnp.sum(shares[...].astype(F32), 0).astype(BF)[None], (64, 8, 128))
 
 
 def spread_kernel(tiles, first, second):
@@ -423,7 +424,7 @@
     (packed,) = call(
         first_grad_kernel,
         (vol, halo) + parts + (slope, second, w2_turned),
-        (((64, 8, 128), F32),),
+        (((64, 8, 128), BF),),
         [pltpu.VMEM((4, 12, 16, 128), BF), pltpu.VMEM((96, 384), BF)],
     )
     shares = lax.all_to_all(packed, BLOCKS, 0, 0)

time: 66.7 us -> 65.5 us (0.982)
  starting transfers between devices: 38.7 us -> 37.4 us
    ppermute x1, starting transfers between devices: 3.19 us -> 1.66 us  [per_device(): rim2 = lax.ppermute(rim0, 'x_hi', SWAP)]
    ppermute x1, waiting for transfers between devices: 0.01 us -> 1.2 us  [per_device(): rim2 = lax.ppermute(rim0, 'x_hi', SWAP)]
    all_to_all x1, waiting for transfers between devices: 11 us -> 9.97 us  [per_device(): shares = lax.all_to_all(packed, BLOCKS, 0, 0)]
  transfers between devices with their start and end apart: 12 -> 12, of which waited for: 3 -> 4; matrix products, arithmetic and copies ran while one was open for 2% -> 2% of each run, Pallas kernels for 9% -> 9%
where the time goes in v4:
time: 65.5 us; the launch traced here: 65.2 us
  starting transfers between devices  37.4 us (57%)
  waiting for transfers between devices  14.3 us (22%)
  Pallas kernels  11.4 us (17%)
  local copies, waits for them, and re-layouts  1.39 us (2%)
  between operations  0.73 us (1%)
    pallas_call x7, Pallas kernels, call(): pl.pallas_call(kernel, in_specs=[VMEM] * len(operands), out_specs=tuple((...  11.4 us
    all_to_all x1, waiting for transfers between devices, per_device(): shares = lax.all_to_all(packed, BLOCKS, 0, 0)  9.97 us
    ppermute x1, starting transfers between devices, per_device(): kernels2 = lax.ppermute(kernels0, ('x_lo', 'x_hi'), ACROSS)  8.86 us
    all_to_all x1, starting transfers between devices, per_device(): shares = lax.all_to_all(packed, BLOCKS, 0, 0)  6.79 us
    all_to_all x1, starting transfers between devices, per_device(): tiles = lax.all_to_all(summed, BLOCKS, 0, 0)  4.62 us
    ppermute x1, starting transfers between devices, per_device(): rim3 = lax.ppermute(rim2, 'core', SWAP)  4.58 us
    ppermute x1, starting transfers between devices, per_device(): part2 = lax.ppermute(part0, 'x_hi', SWAP)  3.65 us
    ppermute x1, starting transfers between devices, per_device(): rim1 = lax.ppermute(rim0, 'core', SWAP)  2.57 us
  transfers between devices with their start and end apart: 12, of which 4 were waited for; matrix products, arithmetic and copies ran while one was open for 2% of the time, Pallas kernels for 9%

profile of v4, /device:TPU:1, one launch (start us, length us, event | category | flops | bytes accessed | tf_op | source)
XLA Modules:
  0.0 65.2 jit_solution(6843378822169865877)
XLA Ops:
  0.6 1.5 %shard_map.75 = (bf16[4,8,64,128]{3,2,1,0:T(8,128)(2,1)S(1)}, bf16[60,16,128]{2,1,0:T(8,128)(2,1)S(1)}, bf16[60,16,128]{2,1,0:T(8,128)(2,1)S(1)}, bf16[32,16,128...) custom-call(bf16[64,4,8,128]{3,2,1,0:T(8,128)(2,1)} %volume.1, ...), custom_call_target="tpu_custom_call" | custom-call | tf_op jit(solution)/shard_map/pallas_call | solution.py:365
  2.2 3.6 %collective-permute-start.5 = (bf16[32,16,128]{2,1,0:T(8,128)(2,1)S(1)}, bf16[32,16,128]{2,1,0:T(8,128)(2,1)S(1)}, u32[]{:S(2)}, u32[]{:S(2)}) collective-permute-start(bf16[32,16,128]{2,1,0:T(8,128)(2,1)S(1)} %get-tuple-element.22.part0), channel_id=1, source_target_pairs={{0,2},{2,0},{1,3},{3,1},{4,6},{6,4},{5,7},{7,5},{8,10},{10,8},{9,1... | collective-permute-start | bytes 393224 | tf_op jit(solution)/shard_map/ppermute | solution.py:398
  5.8 1.6 %collective-permute-start = (bf16[60,16,128]{2,1,0:T(8,128)(2,1)S(1)}, bf16[60,16,128]{2,1,0:T(8,128)(2,1)S(1)}, u32[]{:S(2)}, u32[]{:S(2)}) collective-permute-start(bf16[60,16,128]{2,1,0:T(8,128)(2,1)S(1)} %get-tuple-element.20), channel_id=1, source_target_pairs={{0,4},{4,0},{8,12},{12,8},{16,20},{20,16},{24,28},{28,24},{32,36},... | collective-permute-start | bytes 737288 | tf_op jit(solution)/shard_map/ppermute | solution.py:399
  7.4 0.7 %collective-permute-start.1 = (bf16[60,16,128]{2,1,0:T(8,128)(2,1)S(1)}, bf16[60,16,128]{2,1,0:T(8,128)(2,1)S(1)}, u32[]{:S(2)}, u32[]{:S(2)}) collective-permute-start(bf16[60,16,128]{2,1,0:T(8,128)(2,1)S(1)} %get-tuple-element.21), channel_id=1, source_target_pairs={{4,8},{8,4},{12,16},{16,12},{20,24},{24,20},{28,32},{32,28},{36,40... | collective-permute-start | bytes 737288 | tf_op jit(solution)/shard_map/ppermute | solution.py:400
  8.1 1.3 %collective-permute-start.2 = (bf16[50,16,128]{2,1,0:T(8,128)(2,1)S(1)}, bf16[50,16,128]{2,1,0:T(8,128)(2,1)S(1)}, u32[]{:S(2)}, u32[]{:S(2)}) collective-permute-start(bf16[50,16,128]{2,1,0:T(8,128)(2,1)S(1)} %get-tuple-element.24), channel_id=1, source_target_pairs={{0,1},{1,0},{2,3},{3,2},{4,5},{5,4},{6,7},{7,6},{8,9},{9,8},{10,11... | collective-permute-start | bytes 614408 | tf_op jit(solution)/shard_map/ppermute | solution.py:401
  9.4 8.9 %collective-permute-start.3 = (bf16[18,16,128]{2,1,0:T(8,128)(2,1)S(1)}, bf16[18,16,128]{2,1,0:T(8,128)(2,1)S(1)}, u32[]{:S(2)}, u32[]{:S(2)}) collective-permute-start(bf16[18,16,128]{2,1,0:T(8,128)(2,1)S(1)} %get-tuple-element.23.kernels0), channel_id=1, source_target_pairs={{0,130},{2,128},{128,2},{130,0},{1,131},{3,129},{129,3},{131,1},{4... | collective-permute-start | bytes 221192 | tf_op jit(solution)/shard_map/ppermute | solution.py:397
  18.3 0.0 collective-permute-done.5.part2
  18.3 0.4 collective-permute-start.6
  18.7 2.2 %collective-permute-done.3.kernels2 = bf16[18,16,128]{2,1,0:T(8,128)(2,1)S(1)} collective-permute-done((bf16[18,16,128]{2,1,0:T(8,128)(2,1)S(1)}, bf16[18,16,128]{2,1,0:T(8,128)(2,1)S(1)}, u32[]{:S(2)}, u32[]{:S(2)}) %collective-permute-start.3) | collective-permute-done | bytes 73760 | tf_op jit(solution)/shard_map/ppermute | solution.py:397
  20.8 0.7 %collective-permute-start.4 = (bf16[18,16,128]{2,1,0:T(8,128)(2,1)S(1)}, bf16[18,16,128]{2,1,0:T(8,128)(2,1)S(1)}, u32[]{:S(2)}, u32[]{:S(2)}) collective-permute-start(bf16[18,16,128]{2,1,0:T(8,128)(2,1)S(1)} %collective-permute-done.3.kernels2), channel_id=1, source_target_pairs={{0,1},{1,0},{2,3},{3,2},{4,5},{5,4},{6,7},{7,6},{8,9},{9,8},{10,11... | collective-permute-start | bytes 221192 | tf_op jit(solution)/shard_map/ppermute | solution.py:403
  21.5 0.9 %collective-permute-done.4.kernels3 = bf16[18,16,128]{2,1,0:T(8,128)(2,1)S(1)} collective-permute-done((bf16[18,16,128]{2,1,0:T(8,128)(2,1)S(1)}, bf16[18,16,128]{2,1,0:T(8,128)(2,1)S(1)}, u32[]{:S(2)}, u32[]{:S(2)}) %collective-permute-start.4) | collective-permute-done | bytes 73760 | tf_op jit(solution)/shard_map/ppermute | solution.py:403
  22.4 0.0 collective-permute-done.2.kernels1.part1
  22.4 0.0 collective-permute-done.near
  22.4 0.0 collective-permute-done.1.far
  22.4 2.4 %shard_map.76 = (bf16[4,12,64,128]{3,2,1,0:T(8,128)(2,1)}, f32[4,12,64,128]{3,2,1,0:T(8,128)S(1)}, f32[96,384]{1,0:T(8,128)S(1)}, bf16[3,64,192]{2,1,0:T(8,128)(...) custom-call(bf16[4,8,64,128]{3,2,1,0:T(8,128)(2,1)S(1)} %get-tuple-eleme, ...), custom_call_target="tpu_custom_call" | custom-call | tf_op jit(solution)/shard_map/pallas_call | solution.py:365
  24.9 0.0 collective-permute-done.6.part3
  24.9 2.7 %shard_map.79 = bf16[64,8,128]{2,1,0:T(8,128)(2,1)} custom-call(bf16[4,8,64,128]{3,2,1,0:T(8,128)(2,1)S(1)} %get-tuple-element.19.vol, bf16[4,6,64,128]{3,2,1,0:T(8,128)(2,1)S(1)} %get-tuple-element.30.halo, bf16[32,16,128]{2,1,0:T(8,128)(2,1)S(1)} %get-tuple-element.22.part0, bf16[50,16,128]{2,1,0:T(8,128)(2,1)S(1)} %collective-permute-done.2.kernels1.part1, ...), custom_call_target="tpu_custom_call" | custom-call | tf_op jit(solution)/shard_map/pallas_call | solution.py:365
  27.5 6.8 %all-to-all-start = ((bf16[64,8,128]{2,1,0:T(8,128)(2,1)}), bf16[64,8,128]{2,1,0:T(8,128)(2,1)S(1)}, u32[]{:S(2)}, u32[]{:S(2)}) async-start(bf16[64,8,128]{2,1,0:T(8,128)(2,1)} %shard_map.79), calls=%async_computation | async-start | bytes 262144 | tf_op jit(solution)/shard_map/all_to_all | solution.py:430
  34.4 10.0 %all-to-all-done.shares = bf16[64,8,128]{2,1,0:T(8,128)(2,1)S(1)} async-done(((bf16[64,8,128]{2,1,0:T(8,128)(2,1)}), bf16[64,8,128]{2,1,0:T(8,128)(2,1)S(1)}, u32[]{:S(2)}, u32[]{:S(2)}) %all-to-all-start) | async-done | bytes 131104 | tf_op jit(solution)/shard_map/all_to_all | solution.py:430
  44.3 0.7 %shard_map.80 = bf16[64,8,128]{2,1,0:T(8,128)(2,1)} custom-call(bf16[64,8,128]{2,1,0:T(8,128)(2,1)S(1)} %all-to-all-done.shares), custom_call_target="tpu_custom_call" | custom-call | tf_op jit(solution)/shard_map/pallas_call | solution.py:365
  45.1 4.6 %all-to-all-start.1 = ((bf16[64,8,128]{2,1,0:T(8,128)(2,1)}), bf16[64,8,128]{2,1,0:T(8,128)(2,1)S(1)}, u32[]{:S(2)}, u32[]{:S(2)}) async-start(bf16[64,8,128]{2,1,0:T(8,128)(2,1)} %shard_map.80), calls=%async_computation.1 | async-start | bytes 262144 | tf_op jit(solution)/shard_map/all_to_all | solution.py:439
  49.7 1.7 %collective-permute-start.8 = (bf16[24,16,128]{2,1,0:T(8,128)(2,1)S(1)}, bf16[24,16,128]{2,1,0:T(8,128)(2,1)S(1)}, u32[]{:S(2)}, u32[]{:S(2)}) collective-permute-start(bf16[24,16,128]{2,1,0:T(8,128)(2,1)S(1)} %pad_maximum_fusion.rim0), channel_id=1, source_target_pairs={{0,2},{2,0},{1,3},{3,1},{4,6},{6,4},{5,7},{7,5},{8,10},{10,8},{9,1... | collective-permute-start | bytes 294920 | tf_op jit(solution)/shard_map/ppermute | solution.py:406
  51.4 2.6 %collective-permute-start.7 = (bf16[24,16,128]{2,1,0:T(8,128)(2,1)S(1)}, bf16[24,16,128]{2,1,0:T(8,128)(2,1)S(1)}, u32[]{:S(2)}, u32[]{:S(2)}) collective-permute-start(bf16[24,16,128]{2,1,0:T(8,128)(2,1)S(1)} %pad_maximum_fusion.rim0), channel_id=1, source_target_pairs={{0,1},{1,0},{2,3},{3,2},{4,5},{5,4},{6,7},{7,6},{8,9},{9,8},{10,11... | collective-permute-start | bytes 294920 | tf_op jit(solution)/shard_map/ppermute | solution.py:405
  53.9 1.2 %collective-permute-done.8.rim2 = bf16[24,16,128]{2,1,0:T(8,128)(2,1)S(1)} collective-permute-done((bf16[24,16,128]{2,1,0:T(8,128)(2,1)S(1)}, bf16[24,16,128]{2,1,0:T(8,128)(2,1)S(1)}, u32[]{:S(2)}, u32[]{:S(2)}) %collective-permute-start.8) | collective-permute-done | bytes 98336 | tf_op jit(solution)/shard_map/ppermute | solution.py:406
  55.1 4.6 %collective-permute-start.9 = (bf16[24,16,128]{2,1,0:T(8,128)(2,1)S(1)}, bf16[24,16,128]{2,1,0:T(8,128)(2,1)S(1)}, u32[]{:S(2)}, u32[]{:S(2)}) collective-permute-start(bf16[24,16,128]{2,1,0:T(8,128)(2,1)S(1)} %collective-permute-done.8.rim2), channel_id=1, source_target_pairs={{0,1},{1,0},{2,3},{3,2},{4,5},{5,4},{6,7},{7,6},{8,9},{9,8},{10,11... | collective-permute-start | bytes 294920 | tf_op jit(solution)/shard_map/ppermute | solution.py:407
  59.7 1.6 %shard_map.77 = bf16[4,8,16,128]{3,2,1,0:T(8,128)(2,1)S(1)} custom-call(bf16[4,12,64,128]{3,2,1,0:T(8,128)(2,1)} %get-tuple-element.25.hidden, bf16[96,384]{1,0:T(8,128)(2,1)S(1)} %get-tuple-element.26.w2_own), custom_call_target="tpu_custom_call" | custom-call | tf_op jit(solution)/shard_map/pallas_call | solution.py:365
  61.4 0.7 %copy.8 = bf16[16,4,8,128]{3,2,1,0:T(8,128)(2,1)} copy(bf16[16,4,8,128]{3,0,2,1:T(8,128)(2,1)S(1)} %bitcast.3) | data formatting | bytes 262144
  62.1 0.0 collective-permute-done.7.rim1
  62.1 0.0 collective-permute-done.9.rim3
  62.1 1.7 %shard_map.78 = bf16[4,8,16,128]{3,2,1,0:T(8,128)(2,1)S(1)} custom-call(bf16[32,16,128]{2,1,0:T(8,128)(2,1)S(1)} %get-tuple-element.22.part0, bf16[50,16,128]{2,1,0:T(8,128)(2,1)S(1)} %collective-permute-done.2.kernels1.part1, bf16[32,16,128]{2,1,0:T(8,128)(2,1)S(1)} %collective-permute-done.5.part2, bf16[32,16,128]{2,1,0:T(8,128)(2,1)S(1)} %collective-permute-done.6.part3, ...), custom_call_target="tpu_custom_call" | custom-call | tf_op jit(solution)/shard_map/pallas_call | solution.py:365
  63.7 0.7 %copy.9 = bf16[16,4,8,128]{3,2,1,0:T(8,128)(2,1)} copy(bf16[16,4,8,128]{3,0,2,1:T(8,128)(2,1)S(1)} %bitcast.2) | data formatting | bytes 262144
  64.4 0.8 %shard_map.81 = (f32[3,3,16,64]{3,2,1,0:T(8,128)}, f32[3,3,3,16,64]{4,3,2,1,0:T(8,128)}) custom-call(bf16[64,8,128]{2,1,0:T(8,128)(2,1)S(1)} %all-to-all-done.1.tiles), custom_call_target="tpu_custom_call" | custom-call | tf_op jit(solution)/shard_map/pallas_call | solution.py:365
  (4 shorter events, 0.0 us)
Async XLA Ops:
  2.2 16.1 %collective-permute-start.5 = (bf16[32,16,128]{2,1,0:T(8,128)(2,1)S(1)}, bf16[32,16,128]{2,1,0:T(8,128)(2,1)S(1)}, u32[]{:S(2)}, u32[]{:S(2)}) collective-permute-start(bf16[32,16,128]{2,1,0:T(8,128)(2,1)S(1)} %get-tuple-element.22.part0), channel_id=1, source_target_pairs={{0,2},{2,0},{1,3},{3,1},{4,6},{6,4},{5,7},{7,5},{8,10},{10,8},{9,1... | collective-permute-start | bytes 393224 | tf_op jit(solution)/shard_map/ppermute | solution.py:398
  5.8 16.6 %collective-permute-start = (bf16[60,16,128]{2,1,0:T(8,128)(2,1)S(1)}, bf16[60,16,128]{2,1,0:T(8,128)(2,1)S(1)}, u32[]{:S(2)}, u32[]{:S(2)}) collective-permute-start(bf16[60,16,128]{2,1,0:T(8,128)(2,1)S(1)} %get-tuple-element.20), channel_id=1, source_target_pairs={{0,4},{4,0},{8,12},{12,8},{16,20},{20,16},{24,28},{28,24},{32,36},... | collective-permute-start | bytes 737288 | tf_op jit(solution)/shard_map/ppermute | solution.py:399
  7.4 15.0 %collective-permute-start.1 = (bf16[60,16,128]{2,1,0:T(8,128)(2,1)S(1)}, bf16[60,16,128]{2,1,0:T(8,128)(2,1)S(1)}, u32[]{:S(2)}, u32[]{:S(2)}) collective-permute-start(bf16[60,16,128]{2,1,0:T(8,128)(2,1)S(1)} %get-tuple-element.21), channel_id=1, source_target_pairs={{4,8},{8,4},{12,16},{16,12},{20,24},{24,20},{28,32},{32,28},{36,40... | collective-permute-start | bytes 737288 | tf_op jit(solution)/shard_map/ppermute | solution.py:400
  8.1 14.3 %collective-permute-start.2 = (bf16[50,16,128]{2,1,0:T(8,128)(2,1)S(1)}, bf16[50,16,128]{2,1,0:T(8,128)(2,1)S(1)}, u32[]{:S(2)}, u32[]{:S(2)}) collective-permute-start(bf16[50,16,128]{2,1,0:T(8,128)(2,1)S(1)} %get-tuple-element.24), channel_id=1, source_target_pairs={{0,1},{1,0},{2,3},{3,2},{4,5},{5,4},{6,7},{7,6},{8,9},{9,8},{10,11... | collective-permute-start | bytes 614408 | tf_op jit(solution)/shard_map/ppermute | solution.py:401
  9.4 11.4 %collective-permute-start.3 = (bf16[18,16,128]{2,1,0:T(8,128)(2,1)S(1)}, bf16[18,16,128]{2,1,0:T(8,128)(2,1)S(1)}, u32[]{:S(2)}, u32[]{:S(2)}) collective-permute-start(bf16[18,16,128]{2,1,0:T(8,128)(2,1)S(1)} %get-tuple-element.23.kernels0), channel_id=1, source_target_pairs={{0,130},{2,128},{128,2},{130,0},{1,131},{3,129},{129,3},{131,1},{4... | collective-permute-start | bytes 221192 | tf_op jit(solution)/shard_map/ppermute | solution.py:397
  18.3 6.6 %collective-permute-start.6 = (bf16[32,16,128]{2,1,0:T(8,128)(2,1)S(1)}, bf16[32,16,128]{2,1,0:T(8,128)(2,1)S(1)}, u32[]{:S(2)}, u32[]{:S(2)}) collective-permute-start(bf16[32,16,128]{2,1,0:T(8,128)(2,1)S(1)} %collective-permute-done.5.part2), channel_id=1, source_target_pairs={{0,1},{1,0},{2,3},{3,2},{4,5},{5,4},{6,7},{7,6},{8,9},{9,8},{10,11... | collective-permute-start | bytes 393224 | tf_op jit(solution)/shard_map/ppermute | solution.py:402
  20.8 1.6 %collective-permute-start.4 = (bf16[18,16,128]{2,1,0:T(8,128)(2,1)S(1)}, bf16[18,16,128]{2,1,0:T(8,128)(2,1)S(1)}, u32[]{:S(2)}, u32[]{:S(2)}) collective-permute-start(bf16[18,16,128]{2,1,0:T(8,128)(2,1)S(1)} %collective-permute-done.3.kernels2), channel_id=1, source_target_pairs={{0,1},{1,0},{2,3},{3,2},{4,5},{5,4},{6,7},{7,6},{8,9},{9,8},{10,11... | collective-permute-start | bytes 221192 | tf_op jit(solution)/shard_map/ppermute | solution.py:403
  27.5 16.8 %all-to-all-start = ((bf16[64,8,128]{2,1,0:T(8,128)(2,1)}), bf16[64,8,128]{2,1,0:T(8,128)(2,1)S(1)}, u32[]{:S(2)}, u32[]{:S(2)}) async-start(bf16[64,8,128]{2,1,0:T(8,128)(2,1)} %shard_map.79), calls=%async_computation | async-start | bytes 262144 | tf_op jit(solution)/shard_map/all_to_all | solution.py:430
  45.1 19.4 %all-to-all-start.1 = ((bf16[64,8,128]{2,1,0:T(8,128)(2,1)}), bf16[64,8,128]{2,1,0:T(8,128)(2,1)S(1)}, u32[]{:S(2)}, u32[]{:S(2)}) async-start(bf16[64,8,128]{2,1,0:T(8,128)(2,1)} %shard_map.80), calls=%async_computation.1 | async-start | bytes 262144 | tf_op jit(solution)/shard_map/all_to_all | solution.py:439
  49.7 5.4 %collective-permute-start.8 = (bf16[24,16,128]{2,1,0:T(8,128)(2,1)S(1)}, bf16[24,16,128]{2,1,0:T(8,128)(2,1)S(1)}, u32[]{:S(2)}, u32[]{:S(2)}) collective-permute-start(bf16[24,16,128]{2,1,0:T(8,128)(2,1)S(1)} %pad_maximum_fusion.rim0), channel_id=1, source_target_pairs={{0,2},{2,0},{1,3},{3,1},{4,6},{6,4},{5,7},{7,5},{8,10},{10,8},{9,1... | collective-permute-start | bytes 294920 | tf_op jit(solution)/shard_map/ppermute | solution.py:406
  51.4 10.7 %collective-permute-start.7 = (bf16[24,16,128]{2,1,0:T(8,128)(2,1)S(1)}, bf16[24,16,128]{2,1,0:T(8,128)(2,1)S(1)}, u32[]{:S(2)}, u32[]{:S(2)}) collective-permute-start(bf16[24,16,128]{2,1,0:T(8,128)(2,1)S(1)} %pad_maximum_fusion.rim0), channel_id=1, source_target_pairs={{0,1},{1,0},{2,3},{3,2},{4,5},{5,4},{6,7},{7,6},{8,9},{9,8},{10,11... | collective-permute-start | bytes 294920 | tf_op jit(solution)/shard_map/ppermute | solution.py:405
  55.1 6.9 %collective-permute-start.9 = (bf16[24,16,128]{2,1,0:T(8,128)(2,1)S(1)}, bf16[24,16,128]{2,1,0:T(8,128)(2,1)S(1)}, u32[]{:S(2)}, u32[]{:S(2)}) collective-permute-start(bf16[24,16,128]{2,1,0:T(8,128)(2,1)S(1)} %collective-permute-done.8.rim2), channel_id=1, source_target_pairs={{0,1},{1,0},{2,3},{3,2},{4,5},{5,4},{6,7},{7,6},{8,9},{9,8},{10,11... | collective-permute-start | bytes 294920 | tf_op jit(solution)/shard_map/ppermute | solution.py:407
